TPU v7x, 256 devices: a whole 4x4x8 slice. The times are simulated.
256 devices in a mesh: dp: 4 (over y), seq: 16 (over z, core), mp: 4 (over x).
Axes of the slice: x: 4, y: 4, z: 8, core: 2. Of those that a mesh axis runs over, the one named last changes fastest.
Arguments:
- q_self: bfloat16 [4, 1024, 4096], P('dp', 'seq', 'mp'), may hold values from -12 to 12
- k_self: bfloat16 [4, 1024, 4096], P('dp', 'seq', 'mp'), may hold values from -3 to 3
- v_self: bfloat16 [4, 1024, 4096], P('dp', 'seq', 'mp'), may hold values from -0.75 to 0.75
- out_grad_self: bfloat16 [4, 1024, 4096], P('dp', 'seq', 'mp'), may hold values from -6 to 6
- q_cross: bfloat16 [4, 1024, 4096], P('dp', 'seq', 'mp'), may hold values from -12 to 12
- k_cross: bfloat16 [4, 2048, 4096], P('dp', 'seq', 'mp'), may hold values from -3 to 3
- v_cross: bfloat16 [4, 2048, 4096], P('dp', 'seq', 'mp'), may hold values from -0.75 to 0.75
- out_grad_cross: bfloat16 [4, 1024, 4096], P('dp', 'seq', 'mp'), may hold values from -8 to 8
- dec_lengths: int32 [4, 16], P('dp'), may hold values from 1 to 640, as said below
- enc_lengths: int32 [4, 16], P('dp'), may hold values from 1 to 1280, as said below
- rel_bias: float32 [32, 64], P(None, 'mp'), may hold values from -4 to 4
Outputs:
- grad_q_self: bfloat16 [4, 1024, 4096], P('dp', 'seq', 'mp')
- grad_k_self: bfloat16 [4, 1024, 4096], P('dp', 'seq', 'mp')
- grad_v_self: bfloat16 [4, 1024, 4096], P('dp', 'seq', 'mp')
- grad_q_cross: bfloat16 [4, 1024, 4096], P('dp', 'seq', 'mp')
- grad_k_cross: bfloat16 [4, 2048, 4096], P('dp', 'seq', 'mp')
- grad_v_cross: bfloat16 [4, 2048, 4096], P('dp', 'seq', 'mp')
- bias_grad: float32 [32, 64], P(None, 'mp')
Inputs may be any that keep to these rules, and one draw needn't show every extreme that they name: `dec_lengths`: row p lists the decoder lengths of the 16 examples of pack p in order; they sum to 1024 and the largest is exactly 640. `enc_lengths`: row p lists the encoder lengths of the same 16 examples in the same order; they sum to 2048. The example with 640 decoder rows has exactly 1280 encoder rows; every other example has at least as many encoder rows as decoder rows and at most three times as many.
All inputs are finite; a program needn't handle non-finite values.
Results may differ from a plain program's by a relative error of at most 0.039.
Values may be sent and summed in bfloat16 or wider, within the bound.
A program may use at most 128 MiB of HBM per device.

v0:
```python
import math

import jax
import jax.numpy as jnp
from jax import lax
from jax.sharding import PartitionSpec as P

HEAD_DIM = 64
BUCKETS = 32
DISTANCE = 128


def bucket_of(distances):
    exact_count = BUCKETS // 2
    bucketed = jnp.full(distances.shape, exact_count, jnp.int32)
    for level_index in range(1, BUCKETS - exact_count):
        threshold = math.ceil(
            exact_count * (DISTANCE / exact_count) ** (level_index / (BUCKETS - exact_count))
        )
        bucketed = bucketed + (distances >= threshold).astype(jnp.int32)
    return jnp.where(distances < exact_count, distances, bucketed)


def example_ids(total_rows, lengths):
    segment_ends = jnp.cumsum(lengths)
    positions = jnp.arange(total_rows, dtype=jnp.int32)
    return jnp.sum((positions[:, None] >= segment_ends[None, :]).astype(jnp.int32), axis=1)


def distance_table(rel_bias, offset_base, table_span):
    distances = offset_base + jnp.arange(table_span, dtype=jnp.int32)
    buckets = bucket_of(jnp.maximum(distances, 0))
    one_hot = (buckets[None, :] == jnp.arange(rel_bias.shape[0], dtype=jnp.int32)[:, None]).astype(
        jnp.float32
    )
    bias_table = jnp.einsum("bh,bl->hl", rel_bias, one_hot, precision=lax.Precision.HIGHEST)
    return (one_hot, bias_table)


def spread(bias_table, row_count, col_count):
    full_span = row_count + col_count - 1
    leading = bias_table.shape[:-1]
    tiled_rows = jnp.broadcast_to(bias_table[..., None, :], leading + (row_count, full_span))
    flat_rows = tiled_rows.reshape(leading + (row_count * full_span,))
    flat_rows = jnp.pad(flat_rows, [(0, 0)] * len(leading) + [(0, row_count)])
    skewed = flat_rows.reshape(leading + (row_count, full_span + 1))[..., :col_count]
    return skewed[..., ::-1]


def collapse(matrix, row_count, col_count):
    full_span = row_count + col_count - 1
    leading = matrix.shape[:-2]
    flipped = matrix[..., ::-1]
    padded = jnp.pad(flipped, [(0, 0)] * len(leading) + [(0, 0), (0, row_count)])
    flat_rows = padded.reshape(leading + (row_count * (full_span + 1),))[
        ..., : row_count * full_span
    ]
    return jnp.sum(flat_rows.reshape(leading + (row_count, full_span)), axis=-2)


def shard_group(shard_count, row_count):
    group_size = 1
    while group_size < shard_count and (
        shard_count % group_size != 0 or group_size * row_count < 384
    ):
        group_size += 1
    return group_size


def query_side(
    queries,
    out_grads,
    all_keys,
    all_values,
    key_ids,
    query_ids,
    query_start,
    rel_bias,
    block_rows,
    causal,
):
    row_count, head_count, head_size = queries.shape
    block_count = all_keys.shape[0] // block_rows
    query_pos = query_start + jnp.arange(row_count, dtype=jnp.int32)
    block_ids = jnp.arange(block_count, dtype=jnp.int32)

    def scores_of(block_id):
        key_first = block_id * block_rows
        key_block = lax.dynamic_slice_in_dim(all_keys, key_first, block_rows, 0)
        key_block_ids = lax.dynamic_slice_in_dim(key_ids, key_first, block_rows, 0)
        scores = jnp.einsum("thd,uhd->htu", queries, key_block, preferred_element_type=jnp.float32)
        allowed = query_ids[:, None] == key_block_ids[None, :]
        one_hot = jnp.zeros((1, 1), jnp.float32)
        if causal:
            key_pos = key_first + jnp.arange(block_rows, dtype=jnp.int32)
            allowed = allowed & (query_pos[:, None] >= key_pos[None, :])
            one_hot, bias_table = distance_table(
                rel_bias, query_start - key_first - (block_rows - 1), row_count + block_rows - 1
            )
            scores = scores + spread(bias_table, row_count, block_rows)
        return (jnp.where(allowed[None], scores, -1e30), one_hot)

    def stat_step(running, block_id):
        row_high, total_sum = running
        scores, unused_hot = scores_of(block_id)
        new_high = jnp.maximum(row_high, jnp.max(scores, axis=2))
        total_sum = total_sum * jnp.exp(row_high - new_high) + jnp.sum(
            jnp.exp(scores - new_high[:, :, None]), axis=2
        )
        return ((new_high, total_sum), None)

    start_state = (
        jnp.full((head_count, row_count), -1e30, jnp.float32),
        jnp.zeros((head_count, row_count), jnp.float32),
    )
    (row_high, total_sum), unused_stats = lax.scan(stat_step, start_state, block_ids)

    def weights_of(scores):
        return jnp.exp(scores - row_high[:, :, None]) / total_sum[:, :, None]

    def out_step(summed, block_id):
        scores, unused_hot = scores_of(block_id)
        narrow_weights = weights_of(scores).astype(jnp.bfloat16)
        value_block = lax.dynamic_slice_in_dim(all_values, block_id * block_rows, block_rows, 0)
        return (
            summed
            + jnp.einsum(
                "htu,uhd->thd", narrow_weights, value_block, preferred_element_type=jnp.float32
            ),
            None,
        )

    summed, unused_outs = lax.scan(
        out_step, jnp.zeros((row_count, head_count, head_size), jnp.float32), block_ids
    )
    outputs = summed.astype(jnp.bfloat16)
    row_delta = jnp.einsum("thd,thd->ht", out_grads, outputs, preferred_element_type=jnp.float32)

    def grad_step(running, block_id):
        query_grad, bias_grad_sum = running
        scores, one_hot = scores_of(block_id)
        weights = weights_of(scores)
        narrow_weights = weights.astype(jnp.bfloat16)
        key_block = lax.dynamic_slice_in_dim(all_keys, block_id * block_rows, block_rows, 0)
        value_block = lax.dynamic_slice_in_dim(all_values, block_id * block_rows, block_rows, 0)
        weight_grads = jnp.einsum(
            "thd,uhd->htu", out_grads, value_block, preferred_element_type=jnp.float32
        )
        score_grads = weights * (weight_grads - row_delta[:, :, None])
        narrow_grads = score_grads.astype(jnp.bfloat16)
        query_grad = query_grad + jnp.einsum(
            "htu,uhd->thd", narrow_grads, key_block, preferred_element_type=jnp.float32
        )
        if causal:
            bias_grad_sum = bias_grad_sum + jnp.einsum(
                "hl,bl->bh",
                collapse(score_grads, row_count, block_rows),
                one_hot,
                precision=lax.Precision.HIGHEST,
            )
        key_term = jnp.einsum(
            "htu,thd->uhd", narrow_grads, queries, preferred_element_type=jnp.float32
        )
        value_term = jnp.einsum(
            "htu,thd->uhd", narrow_weights, out_grads, preferred_element_type=jnp.float32
        )
        grad_term = jnp.concatenate(
            [
                key_term.reshape(block_rows, head_count * head_size),
                value_term.reshape(block_rows, head_count * head_size),
            ],
            axis=1,
        ).astype(jnp.bfloat16)
        return ((query_grad, bias_grad_sum), grad_term)

    grad_state = (
        jnp.zeros((row_count, head_count, head_size), jnp.float32),
        jnp.zeros((rel_bias.shape[0], head_count), jnp.float32),
    )
    (query_grad, bias_grad_sum), grad_terms = lax.scan(grad_step, grad_state, block_ids)
    grad_terms = grad_terms.reshape(block_count * block_rows, 2 * head_count * head_size)
    query_grad = query_grad.astype(jnp.bfloat16).reshape(row_count, head_count * head_size)
    return (query_grad, grad_terms, bias_grad_sum, (row_high, total_sum, row_delta))


def on_device(
    q_self,
    k_self,
    v_self,
    out_grad_self,
    q_cross,
    k_cross,
    v_cross,
    out_grad_cross,
    dec_lengths,
    enc_lengths,
    rel_bias,
):
    seq_count = lax.axis_size("seq")
    seq_place = lax.axis_index("seq")
    dec_rows = q_self.shape[1]
    enc_rows = k_cross.shape[1]
    feature_count = q_self.shape[2]
    head_count = feature_count // HEAD_DIM
    dec_total = dec_rows * seq_count
    enc_total = enc_rows * seq_count
    dec_start = seq_place * dec_rows
    dec_ids = example_ids(dec_total, dec_lengths[0])
    enc_ids = example_ids(enc_total, enc_lengths[0])
    my_dec_ids = lax.dynamic_slice_in_dim(dec_ids, dec_start, dec_rows, 0)

    def split_heads(tensor):
        return tensor.reshape(tensor.shape[0] * tensor.shape[1], head_count, HEAD_DIM)

    gathered = (
        lax.all_gather(k_self, "seq", axis=1, tiled=True),
        lax.all_gather(v_self, "seq", axis=1, tiled=True),
        lax.all_gather(k_cross, "seq", axis=1, tiled=True),
        lax.all_gather(v_cross, "seq", axis=1, tiled=True),
    )
    self_group = shard_group(seq_count, dec_rows)
    cross_group = shard_group(seq_count, enc_rows)
    self_dq, self_terms, self_bias, self_stats = query_side(
        split_heads(q_self),
        split_heads(out_grad_self),
        split_heads(gathered[0]),
        split_heads(gathered[1]),
        dec_ids,
        my_dec_ids,
        dec_start,
        rel_bias,
        self_group * dec_rows,
        True,
    )
    cross_dq, cross_terms, unused_bias, cross_stats = query_side(
        split_heads(q_cross),
        split_heads(out_grad_cross),
        split_heads(gathered[2]),
        split_heads(gathered[3]),
        enc_ids,
        my_dec_ids,
        dec_start,
        rel_bias,
        cross_group * enc_rows,
        False,
    )
    self_sums = lax.psum_scatter(
        self_terms.astype(jnp.float32).astype(jnp.bfloat16), "seq", scatter_dimension=0, tiled=True
    ).astype(jnp.float32)
    cross_sums = lax.psum_scatter(
        cross_terms.astype(jnp.float32).astype(jnp.bfloat16), "seq", scatter_dimension=0, tiled=True
    ).astype(jnp.float32)
    self_key_grad = self_sums[:, :feature_count]
    self_value_grad = self_sums[:, feature_count:]
    cross_key_grad = cross_sums[:, :feature_count]
    cross_value_grad = cross_sums[:, feature_count:]
    bias_total = lax.psum(self_bias, ("dp", "seq"))
    bias_grad = bias_total * (1.0 / math.sqrt(lax.axis_size("dp") * dec_total))
    return (
        self_dq.reshape(1, dec_rows, feature_count),
        self_key_grad.reshape(1, dec_rows, feature_count).astype(jnp.bfloat16),
        self_value_grad.reshape(1, dec_rows, feature_count).astype(jnp.bfloat16),
        cross_dq.reshape(1, dec_rows, feature_count),
        cross_key_grad.reshape(1, enc_rows, feature_count).astype(jnp.bfloat16),
        cross_value_grad.reshape(1, enc_rows, feature_count).astype(jnp.bfloat16),
        bias_grad,
    )


def solution(mesh):
    return jax.shard_map(
        on_device,
        mesh=mesh,
        in_specs=(
            P("dp", "seq", "mp"),
            P("dp", "seq", "mp"),
            P("dp", "seq", "mp"),
            P("dp", "seq", "mp"),
            P("dp", "seq", "mp"),
            P("dp", "seq", "mp"),
            P("dp", "seq", "mp"),
            P("dp", "seq", "mp"),
            P("dp", None),
            P("dp", None),
            P(None, "mp"),
        ),
        out_specs=(
            P("dp", "seq", "mp"),
            P("dp", "seq", "mp"),
            P("dp", "seq", "mp"),
            P("dp", "seq", "mp"),
            P("dp", "seq", "mp"),
            P("dp", "seq", "mp"),
            P(None, "mp"),
        ),
        check_vma=False,
    )
```

profile of v0, /device:TPU:1, one launch (start us, length us, event | category | flops | bytes accessed | tf_op | source)
XLA Modules:
  0.0 452.7 jit_solution(5825784003897655049)
XLA Ops:
  17.9 35.9 %all-gather.5.cloned.1.call-done = bf16[1,1024,1024]{2,1,0:T(8,128)(2,1)} async-done(((bf16[1,64,1024]{2,1,0:T(8,128)(2,1)}), bf16[1,1024,1024]{2,1,0:T(8,128)(2,1)}) %all-gather.5.cloned.1.call-update) | async-done | bytes 2097168 | tf_op jit(solution)/shard_map/all_gather | solution.py:216
  53.8 3.9 copy.70
  57.8 31.9 %while.91 = (s32[]{:T(128)}, f32[16,64]{1,0:T(8,128)S(1)}, f32[16,64]{1,0:T(8,128)S(1)}, s32[64]{0:T(128)S(1)}, s32[2]{0:T(128)S(1)}, /*index=5*/s32[1024]{0:T(1...) while((s32[]{:T(128)}, f32[16,64]{1,0:T(8,128)S(1)}, ...), condition=%wide.region_5.6_spmd.clone.clone.clone, body=%wide.region_2.0_spmd.clone.clone.clone.sunk | while | flops 73413688 | bytes 34665884 | solution.py:116
  59.6 2.5 reshape.719
  63.9 2.4 reshape.720
  67.9 2.5 rev.40
  70.4 2.4 fusion.207
  75.5 2.5 reshape.719
  79.8 2.4 reshape.720
  83.8 2.5 rev.40
  86.4 2.4 fusion.207
  89.6 4.1 all-gather.7.cloned.1.call-done
  93.7 3.9 copy.74
  97.7 34.3 %while.92 = (s32[]{:T(128)}, f32[64,16,64]{0,2,1:T(8,128)}, s32[2]{0:T(128)S(1)}, bf16[1024,16,64]{0,2,1:T(8,128)(2,1)}, s32[64]{0:T(128)S(1)}, /*index=5*/s32[1...) while((s32[]{:T(128)}, f32[64,16,64]{0,2,1:T(8,128)}, ...), condition=%wide.region_7.8_spmd.clone.clone.clone, body=%wide.region_6.7_spmd.clone.clone.clone.sunk | while | flops 140648496 | bytes 34098144 | solution.py:133
  99.6 2.5 reshape.721
  103.9 2.5 reshape.722
  108.0 2.5 rev.41
  110.5 3.4 fusion.213
  116.7 2.5 reshape.721
  119.2 1.9 pad.57
  121.1 2.5 reshape.722
  125.2 2.5 rev.41
  127.7 3.4 fusion.213
  133.1 80.9 %while.93 = (s32[]{:T(128)}, f32[64,16,64]{0,2,1:T(8,128)}, f32[32,16]{0,1:T(8,128)S(1)}, bf16[2,512,2048]{2,1,0:T(8,128)(2,1)}, s32[2]{0:T(128)S(1)}, /*index=5...) while((s32[]{:T(128)}, f32[64,16,64]{0,2,1:T(8,128)}, ...), condition=%wide.region_10.11_spmd.clone.clone.clone, body=%wide.region_8.10_spmd.clone.clone.clone.sunk | while | flops 353446976 | bytes 101543680 | solution.py:180
  135.1 2.5 reshape.723
  139.4 2.5 reshape.724
  143.5 2.5 rev.42
  146.0 2.8 fusion.226
  153.4 2.3 convolution_convert_fusion.11
  155.8 2.5 rev.43
  159.7 2.4 copy.117
  162.1 1.9 pad.61
  164.0 2.3 reshape.725
  166.3 3.8 reshape.726
  170.5 3.3 constant_dynamic-update-slice_fusion.5
  175.6 2.5 reshape.723
  179.9 2.5 reshape.724
  184.0 2.5 rev.42
  186.4 2.7 fusion.226
  193.8 2.3 convolution_convert_fusion.11
  196.1 2.5 rev.43
  200.0 2.4 copy.117
  202.4 1.9 pad.61
  204.3 2.3 reshape.725
  206.6 3.7 reshape.726
  210.7 3.3 constant_dynamic-update-slice_fusion.5
  214.1 6.7 %copy.79 = bf16[1,2048,1024]{1,2,0:T(8,128)(2,1)} copy(bf16[1,2048,1024]{2,1,0:T(8,128)(2,1)} %all-gather.9.cloned.1.call-done) | data formatting | bytes 8388608 | tf_op jit(solution)/shard_map/all_gather | solution.py:218
  220.9 15.2 %while.88 = (s32[]{:T(128)}, f32[16,64]{1,0:T(8,128)S(1)}, f32[16,64]{1,0:T(8,128)S(1)}, s32[64]{0:T(128)S(1)}, s32[4]{0:T(128)S(1)}, /*index=5*/s32[2048]{0:T(1...) while((s32[]{:T(128)}, f32[16,64]{1,0:T(8,128)S(1)}, ...), condition=%wide.region_17.18_spmd.clone, body=%wide.region_14.17_spmd.clone.sunk | while | flops 69768200 | bytes 5532106 | solution.py:116
  236.1 6.6 %copy.83 = bf16[1,2048,1024]{1,2,0:T(8,128)(2,1)} copy(bf16[1,2048,1024]{2,1,0:T(8,128)(2,1)} %all-gather.11.cloned.1.call-done) | data formatting | bytes 8388608 | tf_op jit(solution)/shard_map/all_gather | solution.py:219
  242.8 16.1 %while.89 = (s32[]{:T(128)}, f32[64,16,64]{0,2,1:T(8,128)S(1)}, s32[4]{0:T(128)S(1)}, bf16[2048,16,64]{0,2,1:T(8,128)(2,1)}, s32[64]{0:T(128)S(1)}, /*index=5*/s...) while((s32[]{:T(128)}, f32[64,16,64]{0,2,1:T(8,128)S(1)}, ...), condition=%wide.region_19.20_spmd.clone, body=%wide.region_18.19_spmd.clone.sunk | while | flops 136478720 | bytes 2834388 | solution.py:133
  244.2 2.6 fusion.191
  248.3 2.6 fusion.191
  252.3 2.6 fusion.191
  256.3 2.6 fusion.191
  259.0 54.1 %while.90 = (s32[]{:T(128)}, f32[64,16,64]{0,2,1:T(8,128)S(1)}, bf16[4,512,2048]{2,1,0:T(8,128)(2,1)}, s32[4]{0:T(128)S(1)}, bf16[2048,16,64]{0,2,1:T(8,128)(2,1...) while((s32[]{:T(128)}, f32[64,16,64]{0,2,1:T(8,128)S(1)}, ...), condition=%wide.region_21.22_spmd.clone, body=%wide.region_20.21_spmd.clone.sunk | while | flops 344621056 | bytes 28396028 | solution.py:180
  260.5 1.9 fusion.202
  268.2 2.9 copy.116
  274.0 1.9 fusion.202
  281.7 2.9 copy.116
  287.5 1.9 fusion.202
  295.2 2.9 copy.116
  301.0 1.9 fusion.202
  308.6 2.9 copy.116
  315.0 125.9 %psum.7 = f32[32,16]{0,1:T(8,128)S(1)} all-reduce(f32[32,16]{0,1:T(8,128)S(1)} %get-tuple-element.693), channel_id=1, replica_groups=mesh['dp'=4,'seq'=16,'mp'=4] {'dp','seq'}, use_global_device_ids=true, to_apply=%region_23.24 | all-reduce | flops 512 | bytes 4096 | tf_op jit(solution)/shard_map/psum | solution.py:257
  (278 shorter events, 107.6 us)
Async XLA Ops:
  7.2 9.6 %copy-start.19 = (bf16[1,64,1024]{2,1,0:T(8,128)(2,1)S(1)}, bf16[1,64,1024]{2,1,0:T(8,128)(2,1)}, u32[]{:S(2)}) copy-start(bf16[1,64,1024]{2,1,0:T(8,128)(2,1)} %param.27) | copy-start | bytes 393220
  7.2 46.6 %all-gather.5.cloned.1.call-start = ((), (), s32[]{:S(2)}) async-start(), calls=%async_computation.2 | async-start | bytes 2228224 | tf_op jit(solution)/shard_map/all_gather | solution.py:216
  7.9 85.8 %all-gather.7.cloned.1.call-start = ((), (), s32[]{:S(2)}) async-start(), calls=%async_computation.3 | async-start | bytes 2228224 | tf_op jit(solution)/shard_map/all_gather | solution.py:217
  8.7 205.4 %all-gather.9.cloned.1.call-start = ((), (), s32[]{:S(2)}) async-start(), calls=%async_computation.5 | async-start | bytes 4456448 | tf_op jit(solution)/shard_map/all_gather | solution.py:218
  9.4 226.7 %all-gather.11.cloned.1.call-start = ((), (), s32[]{:S(2)}) async-start(), calls=%async_computation.6 | async-start | bytes 4456448 | tf_op jit(solution)/shard_map/all_gather | solution.py:219
  10.0 432.3 %reduce-scatter.3.cloned.1.call-start = ((), (), s32[]{:S(2)}) async-start(), calls=%async_computation.4 | async-start | bytes 4456448 | tf_op jit(solution)/shard_map/reduce_scatter | solution.py:247
  17.0 40.8 %copy-start.7 = (bf16[1,64,1024]{1,2,0:T(8,128)(2,1)}, bf16[1,64,1024]{1,2,0:T(8,128)(2,1)S(1)}, u32[]{:S(2)}) copy-start(bf16[1,64,1024]{1,2,0:T(8,128)(2,1)S(1)} %copy.81) | copy-start | bytes 393220
  17.9 39.8 %copy-start.12 = (f32[32,16]{0,1:T(8,128)S(1)}, f32[32,16]{0,1:T(8,128)}, u32[]{:S(2)}) copy-start(f32[32,16]{0,1:T(8,128)} %param.33) | copy-start | bytes 6148
  66.3 1.6 slice-start
  82.2 1.6 slice-start
  106.4 1.6 slice-start.1
  108.0 2.5 copy-start.15
  113.9 0.8 copy-start.16
  123.5 1.7 slice-start.1
  125.2 2.5 copy-start.15
  131.1 0.8 copy-start.16
  133.3 12.7 %copy-start.9 = (bf16[64,16,64]{0,2,1:T(8,128)(2,1)}, bf16[64,16,64]{0,2,1:T(8,128)(2,1)S(1)}, u32[]{:S(2)}) copy-start(bf16[64,16,64]{0,2,1:T(8,128)(2,1)S(1)} %get-tuple-element.1967) | copy-start | bytes 393220 | tf_op jit(solution)/shard_map/while
  141.9 1.6 slice-start.2
  148.7 1.6 copy-start.2
  150.3 1.6 copy-start
  150.3 1.7 copy-start.3
  152.6 0.8 copy-start.4
  170.5 3.3 copy-start.10
  173.8 12.7 %copy-start.9 = (bf16[64,16,64]{0,2,1:T(8,128)(2,1)}, bf16[64,16,64]{0,2,1:T(8,128)(2,1)S(1)}, u32[]{:S(2)}) copy-start(bf16[64,16,64]{0,2,1:T(8,128)(2,1)S(1)} %get-tuple-element.1967) | copy-start | bytes 393220 | tf_op jit(solution)/shard_map/while
  182.4 1.6 slice-start.2
  189.1 1.6 copy-start.2
  190.7 1.6 copy-start
  190.7 1.7 copy-start.3
  192.9 0.8 copy-start.4
  210.7 3.3 copy-start.10
  214.0 6.9 %copy-start.11 = (bf16[64,16,64]{2,0,1:T(8,128)(2,1)S(1)}, bf16[64,16,64]{2,0,1:T(8,128)(2,1)}, u32[]{:S(2)}) copy-start(bf16[64,16,64]{2,0,1:T(8,128)(2,1)} %copy.82) | copy-start | bytes 393220
  214.0 6.8 %copy-start.13 = (f32[16,64]{1,0:T(8,128)S(1)}, f32[16,64]{1,0:T(8,128)}, u32[]{:S(2)}) copy-start(f32[16,64]{1,0:T(8,128)} %custom-call.5) | copy-start | bytes 12292
  214.0 6.8 %copy-start.17 = (f32[16,64]{1,0:T(8,128)S(1)}, f32[16,64]{1,0:T(8,128)}, u32[]{:S(2)}) copy-start(f32[16,64]{1,0:T(8,128)} %custom-call.6) | copy-start | bytes 12292
  214.0 6.8 %copy-start.18 = (s32[2048]{0:T(1024)S(1)}, s32[2048]{0:T(1024)}, u32[]{:S(2)}) copy-start(s32[2048]{0:T(1024)} %convert_reduce_fusion) | copy-start | bytes 24580
  214.0 229.9 %reduce-scatter.5.cloned.1.call-start = ((), (), s32[]{:S(2)}) async-start(), calls=%async_computation.7 | async-start | bytes 8912896 | tf_op jit(solution)/shard_map/reduce_scatter | solution.py:250
  236.1 6.7 %copy-start.14 = (f32[64,16,64]{0,2,1:T(8,128)S(1)}, f32[64,16,64]{0,2,1:T(8,128)}, u32[]{:S(2)}) copy-start(f32[64,16,64]{0,2,1:T(8,128)} %custom-call.7) | copy-start | bytes 786436
  242.8 16.1 %copy-start.1 = (bf16[1,64,1024]{1,2,0:T(8,128)(2,1)S(1)}, bf16[1,64,1024]{1,2,0:T(8,128)(2,1)}, u32[]{:S(2)}) copy-start(bf16[1,64,1024]{1,2,0:T(8,128)(2,1)} %copy.84) | copy-start | bytes 393220
  242.8 16.2 %copy-start.6 = (f32[64,16,64]{0,2,1:T(8,128)S(1)}, f32[64,16,64]{0,2,1:T(8,128)}, u32[]{:S(2)}) copy-start(f32[64,16,64]{0,2,1:T(8,128)} %custom-call.8) | copy-start | bytes 786436
  242.8 16.2 %copy-start.8 = (bf16[1,64,1024]{1,2,0:T(8,128)(2,1)S(1)}, bf16[1,64,1024]{1,2,0:T(8,128)(2,1)}, u32[]{:S(2)}) copy-start(bf16[1,64,1024]{1,2,0:T(8,128)(2,1)} %copy-done.7) | copy-start | bytes 393220
  313.1 1.0 copy-start.5
Sparse Core Ops, SparseCore 0:
  9.8 43.9 all-gather.4
  55.6 38.0 all-gather.6
  95.6 40.5 all-gather.8
  137.8 40.8 all-gather.10
  214.1 57.9 reduce-scatter.2
  313.2 66.4 reduce-scatter.4
where the time goes:
time: 458 us; the launch traced here: 453 us
  local copies, waits for them, and re-layouts  170 us (37%)
  blocking collectives  126 us (28%)
  matrix products  68 us (15%)
  waiting for transfers between devices  42.6 us (9%)
  other arithmetic  17.8 us (4%)
  between operations  14.5 us (3%)
  loops' own time  13.3 us (3%)
    psum x1, blocking collectives, on_device(): bias_total = lax.psum(self_bias, ('dp', 'seq'))  126 us
    all_gather x1, waiting for transfers between devices, on_device(): lax.all_gather(k_self, 'seq', axis=1, tiled=True)  35.9 us
    dynamic_update_slice x12, local copies, waits for them, and re-layouts, query_side(): lax.scan(grad_step, grad_state, block_ids)  29 us
    dot_general x12, matrix products, scores_of(): jnp.einsum('thd,uhd->htu', queries, key_block, preferred_element_type=jnp...  24.9 us
    dot_general x6, matrix products, out_step(): jnp.einsum('htu,uhd->thd', narrow_weights, value_block, preferred_element...  17.1 us
    rev x6, local copies, waits for them, and re-layouts, spread(): return skewed[..., ::-1]  15.1 us
    reshape x6, local copies, waits for them, and re-layouts, spread(): flat_rows = tiled_rows.reshape(leading + (row_count * full_span,))  14.9 us
    reshape x6, local copies, waits for them, and re-layouts, spread(): flat_rows.reshape(leading + (row_count, full_span + 1))[..., :col_count]  14.6 us
  transfers between devices with their start and end apart: 6, of which 2 were waited for; matrix products, arithmetic and copies ran while one was open for 52% of the time, Pallas kernels for 0%

commit v1 on v0

v1 whole, which is shorter than its diff:
```python
import functools
import math

import jax
import jax.numpy as jnp
from jax import lax
from jax.experimental import pallas as pl
from jax.experimental.pallas import tpu as pltpu
from jax.sharding import PartitionSpec as P

HD = 64
BUCKETS = 32
DISTANCE = 128
NEX = 16
N = 16
DEC = 1024
ENC = 2048
DROW = DEC // N
EROW = ENC // N
BIG = 131072.0
BF = jnp.bfloat16
F32 = jnp.float32
VM = pl.BlockSpec(memory_space=pltpu.VMEM)
SM = pl.BlockSpec(memory_space=pltpu.SMEM)

STEPS = [
    (dz, dc)
    for dz in (3, 5, 4, 2, 6, 1, 7, 0)
    for dc in (0, 1)
    if (dz, dc) != (0, 0)
]


def thresholds():
    half = BUCKETS // 2
    lows = list(range(half + 1))
    for level in range(1, BUCKETS - half):
        lows.append(math.ceil(half * (DISTANCE / half) ** (level / (BUCKETS - half))))
    return lows


LOWS = thresholds()


def swap_halves(x):
    return jnp.concatenate([x[:, HD:], x[:, :HD]], axis=1)


def left_lanes(rows):
    return lax.broadcasted_iota(jnp.int32, (rows, 128), 1) < HD


def dot(a, b):
    return jnp.dot(a, b, preferred_element_type=F32)


def place():
    me = lax.axis_index("seq")
    return me, lax.div(me, 2), lax.rem(me, 2)


def target_of(dz, dc):
    me, z, c = place()
    return lax.rem(z + dz, N // 2) * 2 + lax.rem(c + dc, 2)


def meet(with_dp):
    barrier = pltpu.get_barrier_semaphore()
    for dz, dc in STEPS:
        pl.semaphore_signal(
            barrier,
            inc=1,
            device_id={"seq": target_of(dz, dc)},
            device_id_type=pl.DeviceIdType.MESH,
        )
    if with_dp:
        for k in range(1, 4):
            pl.semaphore_signal(
                barrier,
                inc=1,
                device_id={"dp": lax.rem(lax.axis_index("dp") + k, 4)},
                device_id_type=pl.DeviceIdType.MESH,
            )
    pl.semaphore_wait(barrier, len(STEPS) + (3 if with_dp else 0))


def seq_copy(src, dst, send_sem, recv_sem, which, step):
    dz, dc = step
    return pltpu.make_async_remote_copy(
        src_ref=src,
        dst_ref=dst,
        send_sem=send_sem.at[which, dz * 2 + dc],
        recv_sem=recv_sem.at[which, dz * 2 + dc],
        device_id={"seq": target_of(dz, dc)},
        device_id_type=pl.DeviceIdType.MESH,
    )


def pack_heads(a_ref, b_ref, out_ref):
    rows = a_ref.shape[0]
    left = left_lanes(rows)
    for pair in range(N // 2):
        a = a_ref[:, pair * 128 : pair * 128 + 128]
        b = b_ref[:, pair * 128 : pair * 128 + 128]
        out_ref[2 * pair] = jnp.where(left, a, swap_halves(b))
        out_ref[2 * pair + 1] = jnp.where(left, swap_halves(a), b)


def gather_kernel(
    q_s, k_s, v_s, g_s, q_c, k_c, v_c, g_c, x1, x2, x3, x4, p1, p2, p3, p4, send_sem, recv_sem
):
    me, z, c = place()
    pack_heads(q_s, k_s, p1)
    pack_heads(v_s, g_s, p2)
    pack_heads(q_c, g_c, p3)
    pack_heads(k_c, v_c, p4)
    meet(False)
    copies = []
    for which, (src, dst, rows) in enumerate(
        ((p1, x1, DROW), (p2, x2, DROW), (p3, x3, DROW), (p4, x4, EROW))
    ):
        for step in STEPS:
            copy = seq_copy(
                src.at[target_of(*step)],
                dst.at[pl.ds(me * rows, rows)],
                send_sem,
                recv_sem,
                which,
                step,
            )
            copy.start()
            copies.append(copy)
    for src, dst, rows in ((p1, x1, DROW), (p2, x2, DROW), (p3, x3, DROW), (p4, x4, EROW)):
        dst[pl.ds(me * rows, rows), :] = src[me]
    for copy in copies:
        copy.wait()


def gather_heads(*arrays):
    return pl.pallas_call(
        gather_kernel,
        out_shape=[
            jax.ShapeDtypeStruct((DEC, 128), BF),
            jax.ShapeDtypeStruct((DEC, 128), BF),
            jax.ShapeDtypeStruct((DEC, 128), BF),
            jax.ShapeDtypeStruct((ENC, 128), BF),
        ],
        in_specs=[VM] * 8,
        out_specs=[VM] * 4,
        scratch_shapes=[
            pltpu.VMEM((N, DROW, 128), BF),
            pltpu.VMEM((N, DROW, 128), BF),
            pltpu.VMEM((N, DROW, 128), BF),
            pltpu.VMEM((N, EROW, 128), BF),
            pltpu.SemaphoreType.DMA((4, N)),
            pltpu.SemaphoreType.DMA((4, N)),
        ],
        compiler_params=pltpu.CompilerParams(collective_id=0, has_side_effects=True),
        name="gather_heads",
    )(*arrays)


def scatter_kernel(
    g1, gqs, gqc, g3, bias, r1, rqs, rqc, r3, rb, dp_part, bias_sum, send_sem, recv_sem, dp_sem
):
    me, z, c = place()
    my_dp = lax.axis_index("dp")
    meet(True)
    dp_copies = []
    for k in range(1, 4):
        copy = pltpu.make_async_remote_copy(
            src_ref=bias,
            dst_ref=dp_part.at[my_dp],
            send_sem=dp_sem.at[0, k],
            recv_sem=dp_sem.at[1, k],
            device_id={"dp": lax.rem(my_dp + k, 4)},
            device_id_type=pl.DeviceIdType.MESH,
        )
        copy.start()
        dp_copies.append(copy)
    dp_part[my_dp] = bias[...]
    copies = []
    jobs = ((g1, r1), (gqs, rqs), (g3, r3), (gqc, rqc))
    for which, (src, dst) in enumerate(jobs):
        if which == 2:
            for copy in dp_copies:
                copy.wait()
            total = ((dp_part[0] + dp_part[1]) + dp_part[2]) + dp_part[3]
            bias_sum[...] = total
            rb[me] = total
        for step in STEPS:
            copy = seq_copy(
                src.at[target_of(*step)], dst.at[me], send_sem, recv_sem, which, step
            )
            copy.start()
            copies.append(copy)
    for step in STEPS:
        copy = seq_copy(bias_sum, rb.at[me], send_sem, recv_sem, 4, step)
        copy.start()
        copies.append(copy)
    for src, dst in jobs:
        dst[me] = src[me]
    for copy in copies:
        copy.wait()


def scatter_rows(g1, gqs, gqc, g3, bias):
    return pl.pallas_call(
        scatter_kernel,
        out_shape=[
            jax.ShapeDtypeStruct((N, DROW, 128), BF),
            jax.ShapeDtypeStruct((N, DROW // 2, 128), BF),
            jax.ShapeDtypeStruct((N, DROW // 2, 128), BF),
            jax.ShapeDtypeStruct((N, EROW, 128), BF),
            jax.ShapeDtypeStruct((N, 1, 128), F32),
        ],
        in_specs=[VM] * 5,
        out_specs=[VM] * 5,
        scratch_shapes=[
            pltpu.VMEM((4, 1, 128), F32),
            pltpu.VMEM((1, 128), F32),
            pltpu.SemaphoreType.DMA((5, N)),
            pltpu.SemaphoreType.DMA((5, N)),
            pltpu.SemaphoreType.DMA((2, 4)),
        ],
        compiler_params=pltpu.CompilerParams(collective_id=1, has_side_effects=True),
        name="scatter_rows",
    )(g1, gqs, gqc, g3, bias)


def unpack_kernel(r1, rqs, rqc, r3, rb, dqs, dks, dvs, dqc, dkc, dvc, dbias):
    def pairs(src, key_out, value_out):
        left = left_lanes(src.shape[1])
        for pair in range(N // 2):
            a, b = src[2 * pair], src[2 * pair + 1]
            key_out[:, pair * 128 : pair * 128 + 128] = jnp.where(left, a, swap_halves(b))
            value_out[:, pair * 128 : pair * 128 + 128] = jnp.where(left, swap_halves(a), b)

    def queries(src, out):
        half = src.shape[1]
        left = left_lanes(half)
        for pair in range(N // 2):
            a, b = src[2 * pair], src[2 * pair + 1]
            out[0:half, pair * 128 : pair * 128 + 128] = jnp.where(left, a, swap_halves(b))
            out[half : 2 * half, pair * 128 : pair * 128 + 128] = jnp.where(
                left, swap_halves(a), b
            )

    pairs(r1, dks, dvs)
    pairs(r3, dkc, dvc)
    queries(rqs, dqs)
    queries(rqc, dqc)
    rows = jnp.concatenate([rb[i] for i in range(N)], axis=0)
    turned = jnp.concatenate([rows, jnp.zeros((128 - N, 128), F32)], axis=0).T
    dbias[...] = turned[:BUCKETS, :N] * (1.0 / math.sqrt(4 * DEC))


def unpack(*arrays):
    dec = jax.ShapeDtypeStruct((DROW, N * HD), BF)
    enc = jax.ShapeDtypeStruct((EROW, N * HD), BF)
    return pl.pallas_call(
        unpack_kernel,
        out_shape=[dec, dec, dec, dec, enc, enc, jax.ShapeDtypeStruct((BUCKETS, N), F32)],
        in_specs=[VM] * 5,
        out_specs=[VM] * 7,
        name="unpack",
    )(*arrays)


def ends_of(lengths):
    ends, total = [], jnp.int32(0)
    for e in range(NEX):
        total = total + lengths[0, e]
        ends.append(total)
    return ends


def key_features(ends, out_ref, rows):
    lane = lax.broadcasted_iota(jnp.int32, (1, 128), 1)
    low = jnp.zeros((1, 128), jnp.int32)
    high = jnp.zeros((1, 128), jnp.int32)
    for e in range(NEX):
        if e:
            low = jnp.where(lane == e, ends[e - 1], low)
        high = jnp.where(lane == e, ends[e], high)
    for first in range(0, rows, 256):
        row = lax.broadcasted_iota(jnp.int32, (256, 128), 0) + first
        inside = (row >= low) & (row < high)
        out_ref[first : first + 256, :] = jnp.where(inside, 1.0, 0.0).astype(BF)


def query_features(ends, out_ref):
    col = lax.broadcasted_iota(jnp.int32, (NEX, DEC), 1)
    sub = lax.broadcasted_iota(jnp.int32, (NEX, DEC), 0)
    low = jnp.zeros((NEX, DEC), jnp.int32)
    high = jnp.zeros((NEX, DEC), jnp.int32)
    for e in range(NEX):
        if e:
            low = jnp.where(sub == e, ends[e - 1], low)
        high = jnp.where(sub == e, ends[e], high)
    inside = (col >= low) & (col < high)
    out_ref[0:NEX, :] = jnp.where(inside, 0.0, -BIG).astype(BF)
    out_ref[NEX:128, :] = jnp.zeros((128 - NEX, DEC), BF)


def bias_tiles(rel_bias, head, tile_ref):
    base = lax.broadcasted_iota(jnp.int32, (128, 128), 1) - lax.broadcasted_iota(
        jnp.int32, (128, 128), 0
    )
    last = rel_bias[BUCKETS - 1, head]
    made = []
    for shift in (0, 128):
        distance = base + shift
        tile = jnp.full((128, 128), rel_bias[0, head] - last, F32)
        for b in range(1, BUCKETS):
            tile = jnp.where(distance >= LOWS[b], rel_bias[b, head] - last, tile)
        made.append(jnp.where(distance >= 0, tile, -BIG))
    near, next_one = made
    zero = jnp.zeros((128, 128), F32)
    tile_ref[0:128, 0:128] = zero
    tile_ref[0:128, 128:256] = zero
    tile_ref[128:256, 0:128] = next_one
    tile_ref[128:256, 128:256] = zero
    tile_ref[256:384, 0:128] = near
    tile_ref[256:384, 128:256] = next_one
    tile_ref[384:512, 0:128] = jnp.full((128, 128), -BIG, F32)
    tile_ref[384:512, 128:256] = near


def bucket_sums(near, next_one, far):
    base = lax.broadcasted_iota(jnp.int32, (128, 128), 1) - lax.broadcasted_iota(
        jnp.int32, (128, 128), 0
    )
    lane = lax.broadcasted_iota(jnp.int32, (1, 128), 1)
    out = jnp.zeros((1, 128), F32)
    for b in range(BUCKETS):
        total = jnp.zeros((1, 128), F32)
        for shift, part in ((0, near), (128, next_one)):
            distance = base + shift
            hit = distance >= LOWS[b]
            if b + 1 < BUCKETS:
                hit = hit & (distance < LOWS[b + 1])
            total = total + jnp.sum(jnp.where(hit, part, 0.0), axis=0, keepdims=True)
        if b + 1 == BUCKETS:
            total = total + far
        out = jnp.where(lane == b, jnp.sum(total, axis=1, keepdims=True), out)
    return out


def turn(src_ref, out_ref, rows):
    for first in range(0, rows, 256):
        out_ref[:, first : first + 256] = src_ref[first : first + 256, :].T


def query_out(grad_ref, out_ref):
    left = left_lanes(DROW // 2)
    for first in range(0, DEC, 256):
        part = grad_ref[:, first : first + 256].astype(BF)
        rows = jnp.concatenate([part, part], axis=0).T
        for i in range(256 // DROW):
            a = rows[i * DROW : i * DROW + DROW // 2]
            b = rows[i * DROW + DROW // 2 : (i + 1) * DROW]
            out_ref[first // DROW + i] = jnp.where(left, a, b)


def finish_rows(high_sum, out_t, grad_t):
    inverse = 1.0 / high_sum
    out_t = out_t * inverse
    scaled = (grad_t.astype(F32) * inverse).astype(BF)
    delta = jnp.sum(scaled.astype(F32) * out_t, axis=0, keepdims=True)
    zero = jnp.zeros_like(scaled)
    rows = jnp.concatenate([zero, scaled], axis=0).T
    return scaled, delta, rows


def compute_kernel(
    x1, x2, x3, x4, dec_len, enc_len, rel_bias,
    g1, gqs, gqc, g3, bias_out,
    t1, t2, t3, t4, mk_s, mk_c, mq, tiles, scores, e_s, e_c, sg, delta_ref, rq, rg, dq,
):
    head = lax.axis_index("seq")
    dec_ends = ends_of(dec_len)
    key_features(dec_ends, mk_s, DEC)
    key_features(ends_of(enc_len), mk_c, ENC)
    query_features(dec_ends, mq)
    bias_tiles(rel_bias, head, tiles)
    turn(x1, t1, DEC)
    turn(x2, t2, DEC)
    turn(x3, t3, DEC)
    turn(x4, t4, ENC)
    zeros = jnp.zeros((HD, 256), BF)
    for first in range(0, DEC, 256):
        left = left_lanes(256)
        rq[first : first + 256, :] = jnp.where(left, x1[first : first + 256, :], 0).astype(BF)

    for tb in range(DEC // 256):
        span = slice(tb * 256, tb * 256 + 256)
        right = jnp.concatenate([zeros, t1[0:HD, span], mq[:, span]], axis=0)
        high = jnp.full((1, 256), -4.0 * BIG, F32)
        for cu in range(tb + 1):
            rows = slice(cu * 256, cu * 256 + 256)
            s = dot(jnp.concatenate([x1[rows, :], mk_s[rows, :]], axis=1), right)
            if tb - cu < 2:
                at = 256 * (1 - (tb - cu))
                s = s + tiles[at : at + 256, :]
            scores[rows, :] = s
            high = jnp.maximum(high, jnp.max(s, axis=0, keepdims=True))
        total = jnp.zeros((1, 256), F32)
        out_t = jnp.zeros((HD, 256), F32)
        for cu in range(tb + 1):
            rows = slice(cu * 256, cu * 256 + 256)
            e = jnp.exp(scores[rows, :] - high)
            total = total + jnp.sum(e, axis=0, keepdims=True)
            narrow = e.astype(BF)
            e_s[rows, span] = narrow
            out_t = out_t + dot(t2[0:HD, rows], narrow)
        scaled, delta, rows_g = finish_rows(total, out_t, t2[HD:128, span])
        sg[:, span] = scaled
        delta_ref[:, span] = delta
        rg[span, :] = rows_g

    near = jnp.zeros((128, 128), F32)
    next_one = jnp.zeros((128, 128), F32)
    far = jnp.zeros((1, 128), F32)
    dq[...] = jnp.zeros_like(dq)

    def fold(x):
        x = jnp.sum(x, axis=0, keepdims=True)
        return sum(x[:, i : i + 128] for i in range(0, x.shape[1], 128))

    for cu in range(DEC // 256):
        rows = slice(cu * 256, cu * 256 + 256)
        span = slice(cu * 256, DEC)
        width = DEC - cu * 256
        right = jnp.concatenate([sg[:, span], jnp.zeros((HD, width), BF)], axis=0)
        dp = dot(x2[rows, :], right)
        e = e_s[rows, span]
        ds = e.astype(F32) * (dp - delta_ref[:, span])
        narrow = ds.astype(BF)
        g1_part = dot(narrow, rq[span, :]) + dot(e, rg[span, :])
        for i in range(256 // DROW):
            g1[cu * (256 // DROW) + i] = g1_part[i * DROW : (i + 1) * DROW].astype(BF)
        dq[:, span] += dot(t1[HD:128, rows], narrow)
        near = near + ds[0:128, 0:128] + ds[128:256, 128:256]
        next_one = next_one + ds[0:128, 128:256]
        if width > 256:
            next_one = next_one + ds[128:256, 256:384]
            far = far + fold(ds[0:128, 256:]) + fold(ds[128:256, 384:])
    bias_out[...] = bucket_sums(near, next_one, far)
    query_out(dq, gqs)

    for first in range(0, DEC, 256):
        left = left_lanes(256)
        rq[first : first + 256, :] = jnp.where(left, x3[first : first + 256, :], 0).astype(BF)

    def cross_rows(tb, carry):
        span = pl.ds(pl.multiple_of(tb * 256, 256), 256)
        right = jnp.concatenate([t3[0:HD, span], zeros, mq[:, span]], axis=0)
        high = jnp.full((1, 256), -4.0 * BIG, F32)
        for cu in range(ENC // 256):
            rows = slice(cu * 256, cu * 256 + 256)
            s = dot(jnp.concatenate([x4[rows, :], mk_c[rows, :]], axis=1), right)
            scores[rows, :] = s
            high = jnp.maximum(high, jnp.max(s, axis=0, keepdims=True))
        total = jnp.zeros((1, 256), F32)
        out_t = jnp.zeros((HD, 256), F32)
        for cu in range(ENC // 256):
            rows = slice(cu * 256, cu * 256 + 256)
            e = jnp.exp(scores[rows, :] - high)
            total = total + jnp.sum(e, axis=0, keepdims=True)
            narrow = e.astype(BF)
            e_c[rows, span] = narrow
            out_t = out_t + dot(t4[HD:128, rows], narrow)
        scaled, delta, rows_g = finish_rows(total, out_t, t3[HD:128, span])
        sg[:, span] = scaled
        delta_ref[:, span] = delta
        rg[span, :] = rows_g
        return carry

    lax.fori_loop(0, DEC // 256, cross_rows, 0)
    dq[...] = jnp.zeros_like(dq)

    def cross_keys(cu, carry):
        rows = pl.ds(pl.multiple_of(cu * 256, 256), 256)
        right = jnp.concatenate([jnp.zeros((HD, DEC), BF), sg[...]], axis=0)
        dp = dot(x4[rows, :], right)
        e = e_c[rows, :]
        narrow = (e.astype(F32) * (dp - delta_ref[...])).astype(BF)
        part = dot(narrow, rq[...]) + dot(e, rg[...])
        for i in range(256 // EROW):
            g3[cu * (256 // EROW) + i] = part[i * EROW : (i + 1) * EROW].astype(BF)
        dq[...] += dot(t4[0:HD, rows], narrow)
        return carry

    lax.fori_loop(0, ENC // 256, cross_keys, 0)
    query_out(dq, gqc)


def compute(x1, x2, x3, x4, dec_len, enc_len, rel_bias):
    return pl.pallas_call(
        compute_kernel,
        out_shape=[
            jax.ShapeDtypeStruct((N, DROW, 128), BF),
            jax.ShapeDtypeStruct((N, DROW // 2, 128), BF),
            jax.ShapeDtypeStruct((N, DROW // 2, 128), BF),
            jax.ShapeDtypeStruct((N, EROW, 128), BF),
            jax.ShapeDtypeStruct((1, 128), F32),
        ],
        in_specs=[VM] * 4 + [SM] * 3,
        out_specs=[VM] * 5,
        scratch_shapes=[
            pltpu.VMEM((128, DEC), BF),
            pltpu.VMEM((128, DEC), BF),
            pltpu.VMEM((128, DEC), BF),
            pltpu.VMEM((128, ENC), BF),
            pltpu.VMEM((DEC, 128), BF),
            pltpu.VMEM((ENC, 128), BF),
            pltpu.VMEM((128, DEC), BF),
            pltpu.VMEM((512, 256), F32),
            pltpu.VMEM((ENC, 256), F32),
            pltpu.VMEM((DEC, DEC), BF),
            pltpu.VMEM((ENC, DEC), BF),
            pltpu.VMEM((HD, DEC), BF),
            pltpu.VMEM((1, DEC), F32),
            pltpu.VMEM((DEC, 128), BF),
            pltpu.VMEM((DEC, 128), BF),
            pltpu.VMEM((HD, DEC), F32),
        ],
        name="attention_grads",
    )(x1, x2, x3, x4, dec_len, enc_len, rel_bias)


def on_device(q_s, k_s, v_s, g_s, q_c, k_c, v_c, g_c, dec_len, enc_len, rel_bias):
    flat = [x.reshape(x.shape[1], x.shape[2]) for x in (q_s, k_s, v_s, g_s, q_c, k_c, v_c, g_c)]
    x1, x2, x3, x4 = gather_heads(*flat)
    g1, gqs, gqc, g3, bias = compute(x1, x2, x3, x4, dec_len, enc_len, rel_bias)
    outs = unpack(*scatter_rows(g1, gqs, gqc, g3, bias))
    return tuple(x.reshape((1,) + x.shape) for x in outs[:6]) + (outs[6],)


def solution(mesh):
    rows = P("dp", "seq", "mp")
    return jax.shard_map(
        on_device,
        mesh=mesh,
        in_specs=(rows,) * 8 + (P("dp", None), P("dp", None), P(None, "mp")),
        out_specs=(rows,) * 6 + (P(None, "mp"),),
        check_vma=False,
    )
```

time: 458 us -> 97.3 us (0.21); the launches traced: 453 us -> 97.1 us
  local copies, waits for them, and re-layouts: 170 us -> 2.75 us
  blocking collectives: 126 us -> 0 us
  Pallas kernels: 0 us -> 93.6 us
  matrix products: 68 us -> 0 us
  waiting for transfers between devices: 42.6 us -> 0 us
  other arithmetic: 17.8 us -> 0 us
  between operations: 14.5 us -> 0.66 us
  loops' own time: 13.3 us -> 0 us
    psum x1 -> x0, blocking collectives: 126 us -> none  [on_device(): bias_total = lax.psum(self_bias, ('dp', 'seq'))]
    pallas_call x0 -> x4, Pallas kernels: none -> 93.6 us  [the longest x1 42.1 us: gather_heads(): pl.pallas_call(gather_kernel, out_shape=[jax.ShapeDtypeStruct((DEC, 128),...]
    dot_general x50 -> x0, matrix products: 68 us -> none  [the longest x12 24.9 us: scores_of(): jnp.einsum('thd,uhd->htu', queries, key_block, preferred_element_type=jnp...]
    reshape x16 -> x0, local copies, waits for them, and re-layouts: 41.6 us -> none  [the longest x6 14.9 us: spread(): flat_rows = tiled_rows.reshape(leading + (row_count * full_span,))]
    all_gather x4 -> x0, waiting for transfers between devices: 40 us -> none  [the longest x1 35.9 us: on_device(): lax.all_gather(k_self, 'seq', axis=1, tiled=True)]
    dynamic_update_slice x12 -> x0, local copies, waits for them, and re-layouts: 29 us -> none  [query_side(): lax.scan(grad_step, grad_state, block_ids)]
    all_gather x4 -> x0, local copies, waits for them, and re-layouts: 21.2 us -> none  [the longest x1 6.73 us: on_device(): lax.all_gather(k_cross, 'seq', axis=1, tiled=True)]
    rev x8 -> x0, local copies, waits for them, and re-layouts: 20.1 us -> none  [the longest x6 15.1 us: spread(): return skewed[..., ::-1]]
  transfers between devices with their start and end apart: 6 -> 0, of which waited for: 2 -> 0; matrix products, arithmetic and copies ran while one was open for 52% -> 0% of each run, Pallas kernels for 0% -> 0%
where the time goes in v1:
time: 97.3 us; the launch traced here: 97.1 us
  Pallas kernels  93.6 us (96%)
  local copies, waits for them, and re-layouts  2.75 us (3%)
    pallas_call x1, Pallas kernels, gather_heads(): pl.pallas_call(gather_kernel, out_shape=[jax.ShapeDtypeStruct((DEC, 128),...  42.1 us
    pallas_call x1, Pallas kernels, scatter_rows(): pl.pallas_call(scatter_kernel, out_shape=[jax.ShapeDtypeStruct((N, DROW,...  32.9 us
    pallas_call x1, Pallas kernels, compute(): pl.pallas_call(compute_kernel, out_shape=[jax.ShapeDtypeStruct((N, DROW,...  16.2 us
    unnamed x6, local copies, waits for them, and re-layouts  2.75 us
    pallas_call x1, Pallas kernels, unpack(): pl.pallas_call(unpack_kernel, out_shape=[dec, dec, dec, dec, enc, enc, ja...  2.39 us

profile of v1, /device:TPU:1, one launch (start us, length us, event | category | flops | bytes accessed | tf_op | source)
XLA Modules:
  0.0 97.1 jit_solution(16224332260972540928)
XLA Ops:
  0.6 0.0 copy-start.1
  0.6 0.7 copy-done.1
  1.3 0.7 copy.18.rel_bias
  2.0 42.1 %gather_heads.1 = (bf16[1024,128]{1,0:T(8,128)(2,1)}, bf16[1024,128]{1,0:T(8,128)(2,1)}, bf16[1024,128]{1,0:T(8,128)(2,1)}, bf16[2048,128]{1,0:T(8,128)(2,1)}) custom-call(bf16[64,1024]{1,0:T(8,128)(2,1)} %bitcast.16, bf16[64,1024]{1,0:T(8,128)(2,1)} %bitcast.17, bf16[64,1024]{1,0:T(8,128)(2,1)} %bitcast.18, bf16[64,1024]{1,0:T(8,128)(2,1)} %bitcast.19, ...), custom_call_target="tpu_custom_call" | custom-call | tf_op jit(solution)/shard_map/gather_heads/pallas_call | solution.py:140
  44.1 16.2 %attention_grads.1 = (bf16[16,64,128]{2,1,0:T(8,128)(2,1)}, bf16[16,32,128]{2,1,0:T(8,128)(2,1)}, bf16[16,32,128]{2,1,0:T(8,128)(2,1)}, bf16[16,128,128]{2,1,0:T(8,128)(2,1)}, f32[1,128]{1,0:T(1,128)}) custom-call(bf16[1024,128]{1,0:T(8,128)(2,1)} %get-tuple-element.28.x1, bf16[1024,128]{1,0:T(8,128)(2,1)} %get-tuple-element.29.x2, ...), custom_call_target="tpu_custom_call" | custom-call | tf_op jit(solution)/shard_map/attention_grads/pallas_call | solution.py:500
  60.3 32.9 %scatter_rows.1 = (bf16[16,64,128]{2,1,0:T(8,128)(2,1)}, bf16[16,32,128]{2,1,0:T(8,128)(2,1)}, bf16[16,32,128]{2,1,0:T(8,128)(2,1)}, bf16[16,128,128]{2,1,0:T(8,128)(2,1)}, f32[16,1,128]{2,1,0:T(1,128)}) custom-call(bf16[16,64,128]{2,1,0:T(8,128)(2,1)} %get-tuple-element.32.g1, bf16[16,32,128]{2,1,0:T(8,128)(2,1)} %get-tuple-element.33.gqs, ...), custom_call_target="tpu_custom_call" | custom-call | tf_op jit(solution)/shard_map/scatter_rows/pallas_call | solution.py:208
  93.3 2.4 %unpack.1 = (bf16[64,1024]{1,0:T(8,128)(2,1)}, bf16[64,1024]{1,0:T(8,128)(2,1)}, bf16[64,1024]{1,0:T(8,128)(2,1)}, bf16[64,1024]{1,0:T(8,128)(2,1)}, bf16[128,10...) custom-call(bf16[16,64,128]{2,1,0:T(8,128)(2,1)} %get-tuple-element.37.r1, ...), custom_call_target="tpu_custom_call" | custom-call | tf_op jit(solution)/shard_map/unpack/pallas_call | solution.py:261
  95.7 0.0 copy-start
  95.7 0.7 copy-done
  96.4 0.7 copy.19
Async XLA Ops:
  0.6 0.7 copy-start.1
  95.7 0.7 copy-start

commit v2 on v1

v2 whole, which is shorter than its diff:
```python
import functools
import math

import jax
import jax.numpy as jnp
from jax import lax
from jax.experimental import pallas as pl
from jax.experimental.pallas import tpu as pltpu
from jax.sharding import PartitionSpec as P

HD = 64
BUCKETS = 32
DISTANCE = 128
NEX = 16
N = 16
DEC = 1024
ENC = 2048
DROW = DEC // N
EROW = ENC // N
BIG = 131072.0
BF = jnp.bfloat16
F32 = jnp.float32
VM = pl.BlockSpec(memory_space=pltpu.VMEM)

STEPS = [
    (dz, dc)
    for dz in (3, 5, 4, 2, 6, 1, 7, 0)
    for dc in (0, 1)
    if (dz, dc) != (0, 0)
]


def thresholds():
    half = BUCKETS // 2
    lows = list(range(half + 1))
    for level in range(1, BUCKETS - half):
        lows.append(math.ceil(half * (DISTANCE / half) ** (level / (BUCKETS - half))))
    return lows


LOWS = thresholds()


def swap_halves(x):
    return jnp.concatenate([x[:, HD:], x[:, :HD]], axis=1)


def left_lanes(rows):
    return lax.broadcasted_iota(jnp.int32, (rows, 128), 1) < HD


def dot(a, b):
    return jnp.dot(a, b, preferred_element_type=F32)


def place():
    me = lax.axis_index("seq")
    return me, lax.div(me, 2), lax.rem(me, 2)


def target_of(dz, dc):
    me, z, c = place()
    return lax.rem(z + dz, N // 2) * 2 + lax.rem(c + dc, 2)


def signal_peers():
    barrier = pltpu.get_barrier_semaphore()
    for dz, dc in STEPS:
        pl.semaphore_signal(
            barrier,
            inc=1,
            device_id={"seq": target_of(dz, dc)},
            device_id_type=pl.DeviceIdType.MESH,
        )
    for k in range(1, 4):
        pl.semaphore_signal(
            barrier,
            inc=1,
            device_id={"dp": lax.rem(lax.axis_index("dp") + k, 4)},
            device_id_type=pl.DeviceIdType.MESH,
        )


def wait_peers():
    pl.semaphore_wait(pltpu.get_barrier_semaphore(), len(STEPS) + 3)


def seq_copy(src, dst, send_sem, recv_sem, which, step):
    dz, dc = step
    return pltpu.make_async_remote_copy(
        src_ref=src,
        dst_ref=dst,
        send_sem=send_sem.at[which, dz * 2 + dc],
        recv_sem=recv_sem.at[which, dz * 2 + dc],
        device_id={"seq": target_of(dz, dc)},
        device_id_type=pl.DeviceIdType.MESH,
    )


def pack_heads(a_ref, b_ref, out_ref):
    rows = a_ref.shape[0]
    left = left_lanes(rows)
    for pair in range(N // 2):
        a = a_ref[:, pair * 128 : pair * 128 + 128]
        b = b_ref[:, pair * 128 : pair * 128 + 128]
        out_ref[2 * pair] = jnp.where(left, a, swap_halves(b))
        out_ref[2 * pair + 1] = jnp.where(left, swap_halves(a), b)


def unpack_kernel(r1, rqs, rqc, r3, rb, dqs, dks, dvs, dqc, dkc, dvc, dbias):
    def pairs(src, key_out, value_out):
        left = left_lanes(src.shape[1])
        for pair in range(N // 2):
            a, b = src[2 * pair], src[2 * pair + 1]
            key_out[:, pair * 128 : pair * 128 + 128] = jnp.where(left, a, swap_halves(b))
            value_out[:, pair * 128 : pair * 128 + 128] = jnp.where(left, swap_halves(a), b)

    def queries(src, out):
        half = src.shape[1]
        left = left_lanes(half)
        for pair in range(N // 2):
            a, b = src[2 * pair], src[2 * pair + 1]
            out[0:half, pair * 128 : pair * 128 + 128] = jnp.where(left, a, swap_halves(b))
            out[half : 2 * half, pair * 128 : pair * 128 + 128] = jnp.where(
                left, swap_halves(a), b
            )

    pairs(r1, dks, dvs)
    pairs(r3, dkc, dvc)
    queries(rqs, dqs)
    queries(rqc, dqc)
    rows = jnp.concatenate([rb[i] for i in range(N)], axis=0)
    dbias[...] = rows[:, :BUCKETS] * (1.0 / math.sqrt(4 * DEC))


def unpack(*arrays):
    dec = jax.ShapeDtypeStruct((DROW, N * HD), BF)
    enc = jax.ShapeDtypeStruct((EROW, N * HD), BF)
    return pl.pallas_call(
        unpack_kernel,
        out_shape=[dec, dec, dec, dec, enc, enc, jax.ShapeDtypeStruct((N, BUCKETS), F32)],
        in_specs=[VM] * 5,
        out_specs=[VM] * 7,
        name="unpack",
    )(*arrays)


def iota(shape, axis):
    return lax.broadcasted_iota(jnp.int32, shape, axis)


def bounds_of(length_ref):
    row = jnp.concatenate(
        [length_ref[...].astype(F32), jnp.zeros((1, 128 - NEX), F32)], axis=1
    )
    spread = jnp.broadcast_to(row, (128, 128))
    sub, lane = iota((128, 128), 0), iota((128, 128), 1)
    turned = spread.T
    low_row = jnp.sum(jnp.where(sub < lane, turned, 0.0), axis=0, keepdims=True)
    high_row = jnp.sum(jnp.where(sub <= lane, turned, 0.0), axis=0, keepdims=True)
    low_col = jnp.sum(jnp.where(lane < sub, spread, 0.0), axis=1, keepdims=True)
    high_col = jnp.sum(jnp.where(lane <= sub, spread, 0.0), axis=1, keepdims=True)
    return low_row, high_row, low_col[:NEX], high_col[:NEX]


def key_features(low, high, out_ref, rows):
    low, high = low.astype(jnp.int32), high.astype(jnp.int32)
    for first in range(0, rows, 256):
        row = iota((256, 128), 0) + first
        inside = (row >= low) & (row < high)
        out_ref[first : first + 256, :] = jnp.where(inside, 1.0, 0.0).astype(BF)


def query_features(low, high, out_ref):
    col = iota((NEX, DEC), 1)
    inside = (col >= low.astype(jnp.int32)) & (col < high.astype(jnp.int32))
    out_ref[0:NEX, :] = jnp.where(inside, 0.0, -BIG).astype(BF)
    out_ref[NEX:128, :] = jnp.zeros((128 - NEX, DEC), BF)


def bias_tiles(rel_bias, head, tile_ref):
    base = lax.broadcasted_iota(jnp.int32, (128, 128), 1) - lax.broadcasted_iota(
        jnp.int32, (128, 128), 0
    )
    row = iota((N, BUCKETS), 0)
    table = jnp.sum(jnp.where(row == head, rel_bias[...], 0.0), axis=0, keepdims=True)
    table = table - table[:, BUCKETS - 1 :]
    made = []
    for shift in (0, 128):
        distance = base + shift
        tile = jnp.broadcast_to(table[:, 0:1], (128, 128))
        for b in range(1, BUCKETS):
            tile = jnp.where(distance >= LOWS[b], table[:, b : b + 1], tile)
        made.append(jnp.where(distance >= 0, tile, -BIG))
    near, next_one = made
    zero = jnp.zeros((128, 128), F32)
    tile_ref[0:128, 0:128] = zero
    tile_ref[0:128, 128:256] = zero
    tile_ref[128:256, 0:128] = next_one
    tile_ref[128:256, 128:256] = zero
    tile_ref[256:384, 0:128] = near
    tile_ref[256:384, 128:256] = next_one
    tile_ref[384:512, 0:128] = jnp.full((128, 128), -BIG, F32)
    tile_ref[384:512, 128:256] = near


def bucket_sums(near, next_one, far):
    base = lax.broadcasted_iota(jnp.int32, (128, 128), 1) - lax.broadcasted_iota(
        jnp.int32, (128, 128), 0
    )
    lane = lax.broadcasted_iota(jnp.int32, (1, 128), 1)
    out = jnp.zeros((1, 128), F32)
    for b in range(BUCKETS):
        total = jnp.zeros((1, 128), F32)
        for shift, part in ((0, near), (128, next_one)):
            distance = base + shift
            hit = distance >= LOWS[b]
            if b + 1 < BUCKETS:
                hit = hit & (distance < LOWS[b + 1])
            total = total + jnp.sum(jnp.where(hit, part, 0.0), axis=0, keepdims=True)
        if b + 1 == BUCKETS:
            total = total + far
        out = jnp.where(lane == b, jnp.sum(total, axis=1, keepdims=True), out)
    return out


def turn(src_ref, out_ref, rows):
    for first in range(0, rows, 256):
        out_ref[:, first : first + 256] = src_ref[first : first + 256, :].T


def query_out(grad_ref, out_ref):
    left = left_lanes(DROW // 2)
    for first in range(0, DEC, 256):
        part = grad_ref[:, first : first + 256].astype(BF)
        rows = jnp.concatenate([part, part], axis=0).T
        for i in range(256 // DROW):
            a = rows[i * DROW : i * DROW + DROW // 2]
            b = rows[i * DROW + DROW // 2 : (i + 1) * DROW]
            out_ref[first // DROW + i] = jnp.where(left, a, b)


def finish_rows(high_sum, out_t, grad_t):
    inverse = 1.0 / high_sum
    out_t = out_t * inverse
    scaled = (grad_t.astype(F32) * inverse).astype(BF)
    delta = jnp.sum(scaled.astype(F32) * out_t, axis=0, keepdims=True)
    zero = jnp.zeros_like(scaled)
    rows = jnp.concatenate([zero, scaled], axis=0).T
    return scaled, delta, rows


def self_part(x1, x2, g1, gqs, bias_out, t1, t2, mk_s, mq, tiles, scores, e_s, sg, delta_ref, rq, rg, dq):
    turn(x1, t1, DEC)
    turn(x2, t2, DEC)
    zeros = jnp.zeros((HD, 256), BF)
    for first in range(0, DEC, 256):
        left = left_lanes(256)
        rq[first : first + 256, :] = jnp.where(left, x1[first : first + 256, :], 0).astype(BF)

    for tb in range(DEC // 256):
        span = slice(tb * 256, tb * 256 + 256)
        right = jnp.concatenate([zeros, t1[0:HD, span], mq[:, span]], axis=0)
        high = jnp.full((1, 256), -4.0 * BIG, F32)
        for cu in range(tb + 1):
            rows = slice(cu * 256, cu * 256 + 256)
            s = dot(jnp.concatenate([x1[rows, :], mk_s[rows, :]], axis=1), right)
            if tb - cu < 2:
                at = 256 * (1 - (tb - cu))
                s = s + tiles[at : at + 256, :]
            scores[rows, :] = s
            high = jnp.maximum(high, jnp.max(s, axis=0, keepdims=True))
        total = jnp.zeros((1, 256), F32)
        out_t = jnp.zeros((HD, 256), F32)
        for cu in range(tb + 1):
            rows = slice(cu * 256, cu * 256 + 256)
            e = jnp.exp(scores[rows, :] - high)
            total = total + jnp.sum(e, axis=0, keepdims=True)
            narrow = e.astype(BF)
            e_s[rows, span] = narrow
            out_t = out_t + dot(t2[0:HD, rows], narrow)
        scaled, delta, rows_g = finish_rows(total, out_t, t2[HD:128, span])
        sg[:, span] = scaled
        delta_ref[:, span] = delta
        rg[span, :] = rows_g

    near = jnp.zeros((128, 128), F32)
    next_one = jnp.zeros((128, 128), F32)
    far = jnp.zeros((1, 128), F32)
    dq[...] = jnp.zeros_like(dq)

    def fold(x):
        x = jnp.sum(x, axis=0, keepdims=True)
        return sum(x[:, i : i + 128] for i in range(0, x.shape[1], 128))

    for cu in range(DEC // 256):
        rows = slice(cu * 256, cu * 256 + 256)
        span = slice(cu * 256, DEC)
        width = DEC - cu * 256
        right = jnp.concatenate([sg[:, span], jnp.zeros((HD, width), BF)], axis=0)
        dp = dot(x2[rows, :], right)
        e = e_s[rows, span]
        ds = e.astype(F32) * (dp - delta_ref[:, span])
        narrow = ds.astype(BF)
        part = dot(narrow, rq[span, :]) + dot(e, rg[span, :])
        for i in range(256 // DROW):
            g1[cu * (256 // DROW) + i] = part[i * DROW : (i + 1) * DROW].astype(BF)
        dq[:, span] += dot(t1[HD:128, rows], narrow)
        near = near + ds[0:128, 0:128] + ds[128:256, 128:256]
        next_one = next_one + ds[0:128, 128:256]
        if width > 256:
            next_one = next_one + ds[128:256, 256:384]
            far = far + fold(ds[0:128, 256:]) + fold(ds[128:256, 384:])
    bias_out[...] = bucket_sums(near, next_one, far)
    query_out(dq, gqs)


def cross_rows(x3, x4, t3, t4, mk_c, mq, scores, e_c, sg, delta_ref, rg):
    def block(tb, carry):
        span = pl.ds(pl.multiple_of(tb * 256, 256), 256)
        right = jnp.concatenate([t3[0:HD, span], jnp.zeros((HD, 256), BF), mq[:, span]], axis=0)
        high = jnp.full((1, 256), -4.0 * BIG, F32)
        for cu in range(ENC // 256):
            rows = slice(cu * 256, cu * 256 + 256)
            s = dot(jnp.concatenate([x4[rows, :], mk_c[rows, :]], axis=1), right)
            scores[rows, :] = s
            high = jnp.maximum(high, jnp.max(s, axis=0, keepdims=True))
        total = jnp.zeros((1, 256), F32)
        out_t = jnp.zeros((HD, 256), F32)
        for cu in range(ENC // 256):
            rows = slice(cu * 256, cu * 256 + 256)
            e = jnp.exp(scores[rows, :] - high)
            total = total + jnp.sum(e, axis=0, keepdims=True)
            narrow = e.astype(BF)
            e_c[rows, span] = narrow
            out_t = out_t + dot(t4[HD:128, rows], narrow)
        scaled, delta, rows_g = finish_rows(total, out_t, t3[HD:128, span])
        sg[:, span] = scaled
        delta_ref[:, span] = delta
        rg[span, :] = rows_g
        return carry

    lax.fori_loop(0, DEC // 256, block, 0)


def cross_keys(cu, x4, t4, g3, e_c, sg, delta_ref, rq, rg, dq):
    rows = pl.ds(pl.multiple_of(cu * 256, 256), 256)
    right = jnp.concatenate([jnp.zeros((HD, DEC), BF), sg[...]], axis=0)
    dp = dot(x4[rows, :], right)
    e = e_c[rows, :]
    narrow = (e.astype(F32) * (dp - delta_ref[...])).astype(BF)
    part = dot(narrow, rq[...]) + dot(e, rg[...])
    for i in range(256 // EROW):
        g3[cu * (256 // EROW) + i] = part[i * EROW : (i + 1) * EROW].astype(BF)
    dq[...] += dot(t4[0:HD, rows], narrow)


def fused_kernel(
    q_s, k_s, v_s, g_s, q_c, k_c, v_c, g_c, dec_len, enc_len, rel_bias,
    r1, rqs, rqc, r3, rb,
    aq, ak, av, ag, bq, bk, bv, bg, dec_v, enc_v, rel_v,
    p1, p2, p3, p4, x1, x2, x3, x4, g1, gqs, gqc, g3, bias, dp_part, bias_sum,
    t1, t2, t3, t4, mk_s, mk_c, mq, tiles, scores, e_s, e_c, sg, delta_ref, rq, rg, dq,
    in_sem, send_sem, recv_sem, dp_sem,
):
    me, z, c = place()
    my_dp = lax.axis_index("dp")
    signal_peers()
    loads = []
    pairs = (
        (k_c, bk), (v_c, bv), (q_c, bq), (g_c, bg), (q_s, aq), (k_s, ak), (v_s, av), (g_s, ag),
        (dec_len, dec_v), (enc_len, enc_v), (rel_bias, rel_v),
    )
    for i, (src, dst) in enumerate(pairs):
        load = pltpu.make_async_copy(src, dst, in_sem.at[i])
        load.start()
        loads.append(load)

    def send_all(which, src, dst, rows):
        copies = []
        for step in STEPS:
            slot = dst.at[me] if rows is None else dst.at[pl.ds(me * rows, rows)]
            copy = seq_copy(src.at[target_of(*step)], slot, send_sem, recv_sem, which, step)
            copy.start()
            copies.append(copy)
        return copies

    loads[0].wait()
    loads[1].wait()
    pack_heads(bk, bv, p4)
    loads[2].wait()
    loads[3].wait()
    pack_heads(bq, bg, p3)
    wait_peers()
    sent = []
    in4 = send_all(0, p4, x4, EROW)
    in3 = send_all(1, p3, x3, DROW)
    for load in loads[4:]:
        load.wait()
    pack_heads(aq, ak, p1)
    pack_heads(av, ag, p2)
    x4[pl.ds(me * EROW, EROW), :] = p4[me]
    x3[pl.ds(me * DROW, DROW), :] = p3[me]
    dec_low, dec_high, dec_low_c, dec_high_c = bounds_of(dec_v)
    enc_low, enc_high, unused_low, unused_high = bounds_of(enc_v)
    key_features(dec_low, dec_high, mk_s, DEC)
    in1 = send_all(2, p1, x1, DROW)
    in2 = send_all(3, p2, x2, DROW)
    key_features(enc_low, enc_high, mk_c, ENC)
    query_features(dec_low_c, dec_high_c, mq)
    bias_tiles(rel_v, me, tiles)
    x1[pl.ds(me * DROW, DROW), :] = p1[me]
    x2[pl.ds(me * DROW, DROW), :] = p2[me]

    for copy in in4:
        copy.wait_recv()
    turn(x4, t4, ENC)
    for copy in in3:
        copy.wait_recv()
    turn(x3, t3, DEC)
    for first in range(0, DEC, 256):
        left = left_lanes(256)
        rq[first : first + 256, :] = jnp.where(left, x3[first : first + 256, :], 0).astype(BF)
    cross_rows(x3, x4, t3, t4, mk_c, mq, scores, e_c, sg, delta_ref, rg)
    dq[...] = jnp.zeros_like(dq)
    out3, ready = [], []

    def send_ready():
        for step in ready:
            copy = seq_copy(
                g3.at[target_of(*step)], r3.at[me], send_sem, recv_sem, 4, step
            )
            copy.start()
            out3.append(copy)

    for dz in (4, 3, 5, 2, 6, 1, 7, 0):
        cross_keys(lax.rem(z + dz, N // 2), x4, t4, g3, e_c, sg, delta_ref, rq, rg, dq)
        send_ready()
        ready = [(dz, dc) for dc in (0, 1) if (dz, dc) != (0, 0)]
    query_out(dq, gqc)
    send_ready()
    r3[me] = g3[me]
    rqc[me] = gqc[me]

    for copy in in1 + in2:
        copy.wait_recv()
    outc = send_all(5, gqc, rqc, None)
    self_part(
        x1, x2, g1, gqs, bias, t1, t2, mk_s, mq, tiles, scores, e_s, sg, delta_ref, rq, rg, dq
    )
    dp_copies = []
    for k in range(1, 4):
        copy = pltpu.make_async_remote_copy(
            src_ref=bias,
            dst_ref=dp_part.at[my_dp],
            send_sem=dp_sem.at[0, k],
            recv_sem=dp_sem.at[1, k],
            device_id={"dp": lax.rem(my_dp + k, 4)},
            device_id_type=pl.DeviceIdType.MESH,
        )
        copy.start()
        dp_copies.append(copy)
    dp_part[my_dp] = bias[...]
    out1 = send_all(6, g1, r1, None)
    outs = send_all(7, gqs, rqs, None)
    r1[me] = g1[me]
    rqs[me] = gqs[me]
    for copy in dp_copies:
        copy.wait()
    total = ((dp_part[0] + dp_part[1]) + dp_part[2]) + dp_part[3]
    bias_sum[...] = total
    rb[me] = total
    outb = []
    for step in STEPS:
        copy = seq_copy(bias_sum, rb.at[me], send_sem, recv_sem, 8, step)
        copy.start()
        outb.append(copy)
    for copy in in4 + in3 + in1 + in2:
        copy.wait_send()
    for copy in out3 + outc + out1 + outs + outb:
        copy.wait()


def fused(*arrays):
    vm = pltpu.VMEM
    return pl.pallas_call(
        fused_kernel,
        out_shape=[
            jax.ShapeDtypeStruct((N, DROW, 128), BF),
            jax.ShapeDtypeStruct((N, DROW // 2, 128), BF),
            jax.ShapeDtypeStruct((N, DROW // 2, 128), BF),
            jax.ShapeDtypeStruct((N, EROW, 128), BF),
            jax.ShapeDtypeStruct((N, 1, 128), F32),
        ],
        in_specs=[pl.BlockSpec(memory_space=pl.ANY)] * 11,
        out_specs=[VM] * 5,
        scratch_shapes=[
            *[vm((DROW, N * HD), BF)] * 5,
            *[vm((EROW, N * HD), BF)] * 2,
            vm((DROW, N * HD), BF),
            vm((1, NEX), jnp.int32),
            vm((1, NEX), jnp.int32),
            vm((N, BUCKETS), F32),
            *[vm((N, DROW, 128), BF)] * 3,
            vm((N, EROW, 128), BF),
            *[vm((DEC, 128), BF)] * 3,
            vm((ENC, 128), BF),
            vm((N, DROW, 128), BF),
            *[vm((N, DROW // 2, 128), BF)] * 2,
            vm((N, EROW, 128), BF),
            vm((1, 128), F32),
            vm((4, 1, 128), F32),
            vm((1, 128), F32),
            *[vm((128, DEC), BF)] * 3,
            vm((128, ENC), BF),
            vm((DEC, 128), BF),
            vm((ENC, 128), BF),
            vm((128, DEC), BF),
            vm((512, 256), F32),
            vm((ENC, 256), F32),
            vm((DEC, DEC), BF),
            vm((ENC, DEC), BF),
            vm((HD, DEC), BF),
            vm((1, DEC), F32),
            vm((DEC, 128), BF),
            vm((DEC, 128), BF),
            vm((HD, DEC), F32),
            pltpu.SemaphoreType.DMA((11,)),
            pltpu.SemaphoreType.DMA((9, N)),
            pltpu.SemaphoreType.DMA((9, N)),
            pltpu.SemaphoreType.DMA((2, 4)),
        ],
        compiler_params=pltpu.CompilerParams(collective_id=0, has_side_effects=True),
        name="attention_grads",
    )(*arrays)


def on_device(q_s, k_s, v_s, g_s, q_c, k_c, v_c, g_c, dec_len, enc_len, rel_bias):
    flat = [x.reshape(x.shape[1], x.shape[2]) for x in (q_s, k_s, v_s, g_s, q_c, k_c, v_c, g_c)]
    outs = unpack(*fused(*flat, dec_len, enc_len, rel_bias.T))
    return tuple(x.reshape((1,) + x.shape) for x in outs[:6]) + (outs[6].T,)


def solution(mesh):
    rows = P("dp", "seq", "mp")
    return jax.shard_map(
        on_device,
        mesh=mesh,
        in_specs=(rows,) * 8 + (P("dp", None), P("dp", None), P(None, "mp")),
        out_specs=(rows,) * 6 + (P(None, "mp"),),
        check_vma=False,
    )
```

time: 97.3 us -> 69.2 us (0.71)
  Pallas kernels: 93.6 us -> 68.4 us
  local copies, waits for them, and re-layouts: 2.75 us -> 0 us
    pallas_call x3 -> x1, Pallas kernels: 91.2 us -> 66 us  [fused(): pl.pallas_call(fused_kernel, out_shape=[jax.ShapeDtypeStruct((N, DROW, 12...]
    unnamed x6 -> x0, local copies, waits for them, and re-layouts: 2.75 us -> none
where the time goes in v2:
time: 69.2 us; the launch traced here: 69.1 us
  Pallas kernels  68.4 us (99%)
    pallas_call x1, Pallas kernels, fused(): pl.pallas_call(fused_kernel, out_shape=[jax.ShapeDtypeStruct((N, DROW, 12...  66 us
    pallas_call x1, Pallas kernels, unpack(): pl.pallas_call(unpack_kernel, out_shape=[dec, dec, dec, dec, enc, enc, ja...  2.4 us

profile of v2, /device:TPU:1, one launch (start us, length us, event | category | flops | bytes accessed | tf_op | source)
XLA Modules:
  0.0 69.1 jit_solution(5859773442276905238)
XLA Ops:
  0.6 66.0 %attention_grads.1 = (bf16[16,64,128]{2,1,0:T(8,128)(2,1)}, bf16[16,32,128]{2,1,0:T(8,128)(2,1)}, bf16[16,32,128]{2,1,0:T(8,128)(2,1)}, bf16[16,128,128]{2,1,0:T(8,128)(2,1)}, f32[16,1,128]{2,1,0:T(1,128)}) custom-call(bf16[64,1024]{1,0:T(8,128)(2,1)} %bitcast.18, bf16[64,1024]{1,0:T(8,128)(2,1)} %bitcast.19, bf16[64,1024]{1,0:T(8,128)(2,1)} %bitcast.20, ...), custom_call_target="tpu_custom_call" | custom-call | tf_op jit(solution)/shard_map/attention_grads/pallas_call | solution.py:486
  66.7 2.4 %unpack.1 = (bf16[64,1024]{1,0:T(8,128)(2,1)}, bf16[64,1024]{1,0:T(8,128)(2,1)}, bf16[64,1024]{1,0:T(8,128)(2,1)}, bf16[64,1024]{1,0:T(8,128)(2,1)}, bf16[128,10...) custom-call(bf16[16,64,128]{2,1,0:T(8,128)(2,1)} %get-tuple-element.19.r1, ...), custom_call_target="tpu_custom_call" | custom-call | tf_op jit(solution)/shard_map/unpack/pallas_call | solution.py:139

commit v3 on v2

--- a/solution.py
+++ b/solution.py
@@ -97,38 +97,32 @@
     )
 
 
-def pack_heads(a_ref, b_ref, out_ref):
+def pack_heads(a_ref, b_ref, out_ref, first):
     rows = a_ref.shape[0]
     left = left_lanes(rows)
+    span = slice(first, first + rows)
     for pair in range(N // 2):
         a = a_ref[:, pair * 128 : pair * 128 + 128]
         b = b_ref[:, pair * 128 : pair * 128 + 128]
-        out_ref[2 * pair] = jnp.where(left, a, swap_halves(b))
-        out_ref[2 * pair + 1] = jnp.where(left, swap_halves(a), b)
-
-
-def unpack_kernel(r1, rqs, rqc, r3, rb, dqs, dks, dvs, dqc, dkc, dvc, dbias):
-    def pairs(src, key_out, value_out):
-        left = left_lanes(src.shape[1])
+        out_ref[2 * pair, span] = jnp.where(left, a, swap_halves(b))
+        out_ref[2 * pair + 1, span] = jnp.where(left, swap_halves(a), b)
+
+
+def unpack_kernel(r3, rs, rb, dqs, dks, dvs, dqc, dkc, dvc, dbias):
+    def spread(src, first, rows, left_out, left_row, right_out, right_row):
+        left = left_lanes(rows)
+        span = slice(first, first + rows)
         for pair in range(N // 2):
-            a, b = src[2 * pair], src[2 * pair + 1]
-            key_out[:, pair * 128 : pair * 128 + 128] = jnp.where(left, a, swap_halves(b))
-            value_out[:, pair * 128 : pair * 128 + 128] = jnp.where(left, swap_halves(a), b)
-
-    def queries(src, out):
-        half = src.shape[1]
-        left = left_lanes(half)
-        for pair in range(N // 2):
-            a, b = src[2 * pair], src[2 * pair + 1]
-            out[0:half, pair * 128 : pair * 128 + 128] = jnp.where(left, a, swap_halves(b))
-            out[half : 2 * half, pair * 128 : pair * 128 + 128] = jnp.where(
-                left, swap_halves(a), b
-            )
-
-    pairs(r1, dks, dvs)
-    pairs(r3, dkc, dvc)
-    queries(rqs, dqs)
-    queries(rqc, dqc)
+            a, b = src[2 * pair, span], src[2 * pair + 1, span]
+            lanes = slice(pair * 128, pair * 128 + 128)
+            left_out[left_row : left_row + rows, lanes] = jnp.where(left, a, swap_halves(b))
+            right_out[right_row : right_row + rows, lanes] = jnp.where(left, swap_halves(a), b)
+
+    half = DROW // 2
+    spread(r3, 0, EROW, dkc, 0, dvc, 0)
+    spread(rs, 0, DROW, dks, 0, dvs, 0)
+    spread(rs, DROW, half, dqs, 0, dqs, half)
+    spread(rs, DROW + half, half, dqc, 0, dqc, half)
     rows = jnp.concatenate([rb[i] for i in range(N)], axis=0)
     dbias[...] = rows[:, :BUCKETS] * (1.0 / math.sqrt(4 * DEC))
 
@@ -139,8 +133,9 @@
     return pl.pallas_call(
         unpack_kernel,
         out_shape=[dec, dec, dec, dec, enc, enc, jax.ShapeDtypeStruct((N, BUCKETS), F32)],
-        in_specs=[VM] * 5,
+        in_specs=[VM] * 3,
         out_specs=[VM] * 7,
+        compiler_params=pltpu.CompilerParams(vmem_limit_bytes=16 * 1024 * 1024),
         name="unpack",
     )(*arrays)
 
@@ -224,12 +219,30 @@
     return out
 
 
-def turn(src_ref, out_ref, rows):
-    for first in range(0, rows, 256):
-        out_ref[:, first : first + 256] = src_ref[first : first + 256, :].T
-
-
-def query_out(grad_ref, out_ref):
+class Rows:
+    def __init__(self, ref, first, count):
+        self.ref, self.first, self.count = ref, first, count
+
+    def part(self, index):
+        devices = 256 // self.count
+        block = self.ref[
+            pl.ds(index * devices, devices), self.first : self.first + self.count, :
+        ]
+        return block.reshape(256, 128)
+
+
+def turn(rows, out_ref):
+    for i in range(N * rows.count // 256):
+        out_ref[:, i * 256 : i * 256 + 256] = rows.part(i).T
+
+
+def left_half(rows, out_ref):
+    left = left_lanes(256)
+    for i in range(N * rows.count // 256):
+        out_ref[i * 256 : i * 256 + 256, :] = jnp.where(left, rows.part(i), 0).astype(BF)
+
+
+def query_out(grad_ref, out_ref, row):
     left = left_lanes(DROW // 2)
     for first in range(0, DEC, 256):
         part = grad_ref[:, first : first + 256].astype(BF)
@@ -237,7 +250,7 @@
         for i in range(256 // DROW):
             a = rows[i * DROW : i * DROW + DROW // 2]
             b = rows[i * DROW + DROW // 2 : (i + 1) * DROW]
-            out_ref[first // DROW + i] = jnp.where(left, a, b)
+            out_ref[first // DROW + i, row : row + DROW // 2] = jnp.where(left, a, b)
 
 
 def finish_rows(high_sum, out_t, grad_t):
@@ -250,13 +263,11 @@
     return scaled, delta, rows
 
 
-def self_part(x1, x2, g1, gqs, bias_out, t1, t2, mk_s, mq, tiles, scores, e_s, sg, delta_ref, rq, rg, dq):
-    turn(x1, t1, DEC)
-    turn(x2, t2, DEC)
+def self_part(x1, x2, gs, bias_out, t1, t2, mk_s, mq, tiles, scores, e_s, sg, delta_ref, rq, rg, dq):
+    turn(x1, t1)
+    turn(x2, t2)
     zeros = jnp.zeros((HD, 256), BF)
-    for first in range(0, DEC, 256):
-        left = left_lanes(256)
-        rq[first : first + 256, :] = jnp.where(left, x1[first : first + 256, :], 0).astype(BF)
+    left_half(x1, rq)
 
     for tb in range(DEC // 256):
         span = slice(tb * 256, tb * 256 + 256)
@@ -264,7 +275,7 @@
         high = jnp.full((1, 256), -4.0 * BIG, F32)
         for cu in range(tb + 1):
             rows = slice(cu * 256, cu * 256 + 256)
-            s = dot(jnp.concatenate([x1[rows, :], mk_s[rows, :]], axis=1), right)
+            s = dot(jnp.concatenate([x1.part(cu), mk_s[rows, :]], axis=1), right)
             if tb - cu < 2:
                 at = 256 * (1 - (tb - cu))
                 s = s + tiles[at : at + 256, :]
@@ -298,13 +309,13 @@
         span = slice(cu * 256, DEC)
         width = DEC - cu * 256
         right = jnp.concatenate([sg[:, span], jnp.zeros((HD, width), BF)], axis=0)
-        dp = dot(x2[rows, :], right)
+        dp = dot(x2.part(cu), right)
         e = e_s[rows, span]
         ds = e.astype(F32) * (dp - delta_ref[:, span])
         narrow = ds.astype(BF)
         part = dot(narrow, rq[span, :]) + dot(e, rg[span, :])
         for i in range(256 // DROW):
-            g1[cu * (256 // DROW) + i] = part[i * DROW : (i + 1) * DROW].astype(BF)
+            gs[cu * (256 // DROW) + i, 0:DROW] = part[i * DROW : (i + 1) * DROW].astype(BF)
         dq[:, span] += dot(t1[HD:128, rows], narrow)
         near = near + ds[0:128, 0:128] + ds[128:256, 128:256]
         next_one = next_one + ds[0:128, 128:256]
@@ -312,17 +323,17 @@
             next_one = next_one + ds[128:256, 256:384]
             far = far + fold(ds[0:128, 256:]) + fold(ds[128:256, 384:])
     bias_out[...] = bucket_sums(near, next_one, far)
-    query_out(dq, gqs)
-
-
-def cross_rows(x3, x4, t3, t4, mk_c, mq, scores, e_c, sg, delta_ref, rg):
+    query_out(dq, gs, DROW)
+
+
+def cross_rows(x4, t3, t4, mk_c, mq, scores, e_c, sg, delta_ref, rg):
     def block(tb, carry):
         span = pl.ds(pl.multiple_of(tb * 256, 256), 256)
         right = jnp.concatenate([t3[0:HD, span], jnp.zeros((HD, 256), BF), mq[:, span]], axis=0)
         high = jnp.full((1, 256), -4.0 * BIG, F32)
         for cu in range(ENC // 256):
             rows = slice(cu * 256, cu * 256 + 256)
-            s = dot(jnp.concatenate([x4[rows, :], mk_c[rows, :]], axis=1), right)
+            s = dot(jnp.concatenate([x4.part(cu), mk_c[rows, :]], axis=1), right)
             scores[rows, :] = s
             high = jnp.maximum(high, jnp.max(s, axis=0, keepdims=True))
         total = jnp.zeros((1, 256), F32)
@@ -346,7 +357,7 @@
 def cross_keys(cu, x4, t4, g3, e_c, sg, delta_ref, rq, rg, dq):
     rows = pl.ds(pl.multiple_of(cu * 256, 256), 256)
     right = jnp.concatenate([jnp.zeros((HD, DEC), BF), sg[...]], axis=0)
-    dp = dot(x4[rows, :], right)
+    dp = dot(x4.part(cu), right)
     e = e_c[rows, :]
     narrow = (e.astype(F32) * (dp - delta_ref[...])).astype(BF)
     part = dot(narrow, rq[...]) + dot(e, rg[...])
@@ -357,9 +368,9 @@
 
 def fused_kernel(
     q_s, k_s, v_s, g_s, q_c, k_c, v_c, g_c, dec_len, enc_len, rel_bias,
-    r1, rqs, rqc, r3, rb,
+    r3, rs, rb,
     aq, ak, av, ag, bq, bk, bv, bg, dec_v, enc_v, rel_v,
-    p1, p2, p3, p4, x1, x2, x3, x4, g1, gqs, gqc, g3, bias, dp_part, bias_sum,
+    pc, ps, xc, xs, g3, gs, bias, dp_part, bias_sum,
     t1, t2, t3, t4, mk_s, mk_c, mq, tiles, scores, e_s, e_c, sg, delta_ref, rq, rg, dq,
     in_sem, send_sem, recv_sem, dp_sem,
 ):
@@ -376,78 +387,58 @@
         load.start()
         loads.append(load)
 
-    def send_all(which, src, dst, rows):
+    def send_all(which, src, dst, steps):
         copies = []
-        for step in STEPS:
-            slot = dst.at[me] if rows is None else dst.at[pl.ds(me * rows, rows)]
-            copy = seq_copy(src.at[target_of(*step)], slot, send_sem, recv_sem, which, step)
+        for step in steps:
+            copy = seq_copy(
+                src.at[target_of(*step)], dst.at[me], send_sem, recv_sem, which, step
+            )
             copy.start()
             copies.append(copy)
         return copies
 
-    loads[0].wait()
-    loads[1].wait()
-    pack_heads(bk, bv, p4)
-    loads[2].wait()
-    loads[3].wait()
-    pack_heads(bq, bg, p3)
+    for load in loads[:4]:
+        load.wait()
+    pack_heads(bk, bv, pc, 0)
+    pack_heads(bq, bg, pc, EROW)
     wait_peers()
-    sent = []
-    in4 = send_all(0, p4, x4, EROW)
-    in3 = send_all(1, p3, x3, DROW)
+    in_c = send_all(0, pc, xc, STEPS)
     for load in loads[4:]:
         load.wait()
-    pack_heads(aq, ak, p1)
-    pack_heads(av, ag, p2)
-    x4[pl.ds(me * EROW, EROW), :] = p4[me]
-    x3[pl.ds(me * DROW, DROW), :] = p3[me]
+    pack_heads(aq, ak, ps, 0)
+    pack_heads(av, ag, ps, DROW)
+    xc[me] = pc[me]
+    xs[me] = ps[me]
     dec_low, dec_high, dec_low_c, dec_high_c = bounds_of(dec_v)
     enc_low, enc_high, unused_low, unused_high = bounds_of(enc_v)
     key_features(dec_low, dec_high, mk_s, DEC)
-    in1 = send_all(2, p1, x1, DROW)
-    in2 = send_all(3, p2, x2, DROW)
+    in_s = send_all(1, ps, xs, STEPS)
     key_features(enc_low, enc_high, mk_c, ENC)
     query_features(dec_low_c, dec_high_c, mq)
     bias_tiles(rel_v, me, tiles)
-    x1[pl.ds(me * DROW, DROW), :] = p1[me]
-    x2[pl.ds(me * DROW, DROW), :] = p2[me]
-
-    for copy in in4:
+    x1, x2 = Rows(xs, 0, DROW), Rows(xs, DROW, DROW)
+    x3, x4 = Rows(xc, EROW, DROW), Rows(xc, 0, EROW)
+
+    for copy in in_c:
         copy.wait_recv()
-    turn(x4, t4, ENC)
-    for copy in in3:
-        copy.wait_recv()
-    turn(x3, t3, DEC)
-    for first in range(0, DEC, 256):
-        left = left_lanes(256)
-        rq[first : first + 256, :] = jnp.where(left, x3[first : first + 256, :], 0).astype(BF)
-    cross_rows(x3, x4, t3, t4, mk_c, mq, scores, e_c, sg, delta_ref, rg)
+    turn(x4, t4)
+    turn(x3, t3)
+    left_half(x3, rq)
+    cross_rows(x4, t3, t4, mk_c, mq, scores, e_c, sg, delta_ref, rg)
     dq[...] = jnp.zeros_like(dq)
     out3, ready = [], []
 
-    def send_ready():
-        for step in ready:
-            copy = seq_copy(
-                g3.at[target_of(*step)], r3.at[me], send_sem, recv_sem, 4, step
-            )
-            copy.start()
-            out3.append(copy)
-
     for dz in (4, 3, 5, 2, 6, 1, 7, 0):
         cross_keys(lax.rem(z + dz, N // 2), x4, t4, g3, e_c, sg, delta_ref, rq, rg, dq)
-        send_ready()
+        out3 += send_all(2, g3, r3, ready)
         ready = [(dz, dc) for dc in (0, 1) if (dz, dc) != (0, 0)]
-    query_out(dq, gqc)
-    send_ready()
+    query_out(dq, gs, DROW + DROW // 2)
+    out3 += send_all(2, g3, r3, ready)
     r3[me] = g3[me]
-    rqc[me] = gqc[me]
-
-    for copy in in1 + in2:
+
+    for copy in in_s:
         copy.wait_recv()
-    outc = send_all(5, gqc, rqc, None)
-    self_part(
-        x1, x2, g1, gqs, bias, t1, t2, mk_s, mq, tiles, scores, e_s, sg, delta_ref, rq, rg, dq
-    )
+    self_part(x1, x2, gs, bias, t1, t2, mk_s, mq, tiles, scores, e_s, sg, delta_ref, rq, rg, dq)
     dp_copies = []
     for k in range(1, 4):
         copy = pltpu.make_async_remote_copy(
@@ -461,23 +452,23 @@
         copy.start()
         dp_copies.append(copy)
     dp_part[my_dp] = bias[...]
-    out1 = send_all(6, g1, r1, None)
-    outs = send_all(7, gqs, rqs, None)
-    r1[me] = g1[me]
-    rqs[me] = gqs[me]
+    near = [step for step in STEPS if step[0] in (0, 1, 7)]
+    out_s = send_all(3, gs, rs, [step for step in STEPS if step not in near])
+    rs[me] = gs[me]
     for copy in dp_copies:
         copy.wait()
     total = ((dp_part[0] + dp_part[1]) + dp_part[2]) + dp_part[3]
     bias_sum[...] = total
     rb[me] = total
-    outb = []
+    out_s += send_all(3, gs, rs, near[:2])
     for step in STEPS:
-        copy = seq_copy(bias_sum, rb.at[me], send_sem, recv_sem, 8, step)
+        copy = seq_copy(bias_sum, rb.at[me], send_sem, recv_sem, 4, step)
         copy.start()
-        outb.append(copy)
-    for copy in in4 + in3 + in1 + in2:
+        out_s.append(copy)
+    out_s += send_all(3, gs, rs, near[2:])
+    for copy in in_c + in_s:
         copy.wait_send()
-    for copy in out3 + outc + out1 + outs + outb:
+    for copy in out3 + out_s:
         copy.wait()
 
 
@@ -486,14 +477,12 @@
     return pl.pallas_call(
         fused_kernel,
         out_shape=[
-            jax.ShapeDtypeStruct((N, DROW, 128), BF),
-            jax.ShapeDtypeStruct((N, DROW // 2, 128), BF),
-            jax.ShapeDtypeStruct((N, DROW // 2, 128), BF),
+            jax.ShapeDtypeStruct((N, EROW, 128), BF),
             jax.ShapeDtypeStruct((N, EROW, 128), BF),
             jax.ShapeDtypeStruct((N, 1, 128), F32),
         ],
-        in_specs=[pl.BlockSpec(memory_space=pl.ANY)] * 11,
-        out_specs=[VM] * 5,
+        in_specs=[pl.BlockSpec(memory_space=pltpu.HBM)] * 11,
+        out_specs=[VM] * 3,
         scratch_shapes=[
             *[vm((DROW, N * HD), BF)] * 5,
             *[vm((EROW, N * HD), BF)] * 2,
@@ -501,13 +490,12 @@
             vm((1, NEX), jnp.int32),
             vm((1, NEX), jnp.int32),
             vm((N, BUCKETS), F32),
-            *[vm((N, DROW, 128), BF)] * 3,
+            vm((N, EROW + DROW, 128), BF),
+            vm((N, 2 * DROW, 128), BF),
+            vm((N, EROW + DROW, 128), BF),
+            vm((N, 2 * DROW, 128), BF),
             vm((N, EROW, 128), BF),
-            *[vm((DEC, 128), BF)] * 3,
-            vm((ENC, 128), BF),
-            vm((N, DROW, 128), BF),
-            *[vm((N, DROW // 2, 128), BF)] * 2,
-            vm((N, EROW, 128), BF),
+            vm((N, 2 * DROW, 128), BF),
             vm((1, 128), F32),
             vm((4, 1, 128), F32),
             vm((1, 128), F32),
@@ -526,18 +514,23 @@
             vm((DEC, 128), BF),
             vm((HD, DEC), F32),
             pltpu.SemaphoreType.DMA((11,)),
-            pltpu.SemaphoreType.DMA((9, N)),
-            pltpu.SemaphoreType.DMA((9, N)),
+            pltpu.SemaphoreType.DMA((5, N)),
+            pltpu.SemaphoreType.DMA((5, N)),
             pltpu.SemaphoreType.DMA((2, 4)),
         ],
-        compiler_params=pltpu.CompilerParams(collective_id=0, has_side_effects=True),
+        compiler_params=pltpu.CompilerParams(collective_id=0, has_side_effects=True, vmem_limit_bytes=32 * 1024 * 1024
+        ),
         name="attention_grads",
     )(*arrays)
 
 
 def on_device(q_s, k_s, v_s, g_s, q_c, k_c, v_c, g_c, dec_len, enc_len, rel_bias):
     flat = [x.reshape(x.shape[1], x.shape[2]) for x in (q_s, k_s, v_s, g_s, q_c, k_c, v_c, g_c)]
-    outs = unpack(*fused(*flat, dec_len, enc_len, rel_bias.T))
+    operands = [
+        pltpu.with_memory_space_constraint(x, pltpu.HBM)
+        for x in (*flat, dec_len, enc_len, rel_bias.T)
+    ]
+    outs = unpack(*fused(*operands))
     return tuple(x.reshape((1,) + x.shape) for x in outs[:6]) + (outs[6].T,)
 
 

time: 69.2 us -> 66.2 us (0.957)
  Pallas kernels: 68.4 us -> 65.4 us
    pallas_call x1, Pallas kernels: 66 us -> 64.2 us  [fused(): pl.pallas_call(fused_kernel, out_shape=[jax.ShapeDtypeStruct((N, EROW, 12...]
    pallas_call x1, Pallas kernels: 2.4 us -> 1.2 us  [unpack(): pl.pallas_call(unpack_kernel, out_shape=[dec, dec, dec, dec, enc, enc, ja...]
where the time goes in v3:
time: 66.2 us; the launch traced here: 66.1 us
  Pallas kernels  65.4 us (99%)
    pallas_call x1, Pallas kernels, fused(): pl.pallas_call(fused_kernel, out_shape=[jax.ShapeDtypeStruct((N, EROW, 12...  64.2 us

profile of v3, /device:TPU:1, one launch (start us, length us, event | category | flops | bytes accessed | tf_op | source)
XLA Modules:
  0.0 66.1 jit_solution(2468263075194690537)
XLA Ops:
  0.6 64.2 %attention_grads.1 = (bf16[16,128,128]{2,1,0:T(8,128)(2,1)S(1)}, bf16[16,128,128]{2,1,0:T(8,128)(2,1)S(1)}, f32[16,1,128]{2,1,0:T(1,128)S(1)}) custom-call(bf16[64,1024]{1,0:T(8,128)(2,1)} %bitcast.18, bf16[64,1024]{1,0:T(8,128)(2,1)} %bitcast.19, bf16[64,1024]{1,0:T(8,128)(2,1)} %bitcast.20, bf16[64,1024]{1,0:T(8,128)(2,1)} %bitcast.21, ...), custom_call_target="tpu_custom_call" | custom-call | tf_op jit(solution)/shard_map/attention_grads/pallas_call | solution.py:477
  64.9 1.2 %unpack.1 = (bf16[64,1024]{1,0:T(8,128)(2,1)}, bf16[64,1024]{1,0:T(8,128)(2,1)}, bf16[64,1024]{1,0:T(8,128)(2,1)}, bf16[64,1024]{1,0:T(8,128)(2,1)}, bf16[128,10...) custom-call(bf16[16,128,128]{2,1,0:T(8,128)(2,1)S(1)} %get-tuple-element.17.r3, ...), custom_call_target="tpu_custom_call" | custom-call | tf_op jit(solution)/shard_map/unpack/pallas_call | solution.py:133

commit v4 on v3

--- a/solution.py
+++ b/solution.py
@@ -63,26 +63,46 @@
     return lax.rem(z + dz, N // 2) * 2 + lax.rem(c + dc, 2)
 
 
-def signal_peers():
+def tell(semaphore, device):
+    pl.semaphore_signal(
+        semaphore, inc=1, device_id=device, device_id_type=pl.DeviceIdType.MESH
+    )
+
+
+def dp_peer(shift):
+    return {"dp": lax.rem(lax.axis_index("dp") + shift, 4)}
+
+
+NEAR = [step for step in STEPS if step[0] in (0, 1, N // 2 - 1)]
+
+
+def at_hops(hops):
+    return [step for step in STEPS if step[0] in (hops, N // 2 - hops)]
+
+
+IN_ORDER = NEAR + at_hops(2) + at_hops(3) + at_hops(4)
+
+
+def greet_near():
     barrier = pltpu.get_barrier_semaphore()
-    for dz, dc in STEPS:
-        pl.semaphore_signal(
-            barrier,
-            inc=1,
-            device_id={"seq": target_of(dz, dc)},
-            device_id_type=pl.DeviceIdType.MESH,
-        )
-    for k in range(1, 4):
-        pl.semaphore_signal(
-            barrier,
-            inc=1,
-            device_id={"dp": lax.rem(lax.axis_index("dp") + k, 4)},
-            device_id_type=pl.DeviceIdType.MESH,
-        )
-
-
-def wait_peers():
-    pl.semaphore_wait(pltpu.get_barrier_semaphore(), len(STEPS) + 3)
+    for step in NEAR:
+        tell(barrier, {"seq": target_of(*step)})
+    tell(barrier, dp_peer(1))
+    tell(barrier, dp_peer(3))
+
+
+def wait_near():
+    pl.semaphore_wait(pltpu.get_barrier_semaphore(), len(NEAR) + 2)
+
+
+def pass_on(up_sem, down_sem, hops):
+    tell(up_sem.at[hops], {"seq": target_of(1, 0)})
+    tell(down_sem.at[hops], {"seq": target_of(N // 2 - 1, 0)})
+
+
+def heard(up_sem, down_sem, hops):
+    pl.semaphore_wait(up_sem.at[hops], 1)
+    pl.semaphore_wait(down_sem.at[hops], 1)
 
 
 def seq_copy(src, dst, send_sem, recv_sem, which, step):
@@ -108,7 +128,10 @@
         out_ref[2 * pair + 1, span] = jnp.where(left, swap_halves(a), b)
 
 
-def unpack_kernel(r3, rs, rb, dqs, dks, dvs, dqc, dkc, dvc, dbias):
+def unpack_kernel(
+    r3, rs, rb, dqs, dks, dvs, dqc, dkc, dvc, dbias,
+    aqs, aks, avs, aqc, akc, avc, abias, sems,
+):
     def spread(src, first, rows, left_out, left_row, right_out, right_row):
         left = left_lanes(rows)
         span = slice(first, first + rows)
@@ -118,23 +141,37 @@
             left_out[left_row : left_row + rows, lanes] = jnp.where(left, a, swap_halves(b))
             right_out[right_row : right_row + rows, lanes] = jnp.where(left, swap_halves(a), b)
 
+    def leave(*which):
+        for i in which:
+            pltpu.make_async_copy(made[i], outs[i], sems.at[i]).start()
+
     half = DROW // 2
-    spread(r3, 0, EROW, dkc, 0, dvc, 0)
-    spread(rs, 0, DROW, dks, 0, dvs, 0)
-    spread(rs, DROW, half, dqs, 0, dqs, half)
-    spread(rs, DROW + half, half, dqc, 0, dqc, half)
+    outs = (dqs, dks, dvs, dqc, dkc, dvc, dbias)
+    made = (aqs, aks, avs, aqc, akc, avc, abias)
+    spread(r3, 0, EROW, akc, 0, avc, 0)
+    leave(4, 5)
+    spread(rs, 0, DROW, aks, 0, avs, 0)
+    leave(1, 2)
     rows = jnp.concatenate([rb[i] for i in range(N)], axis=0)
-    dbias[...] = rows[:, :BUCKETS] * (1.0 / math.sqrt(4 * DEC))
+    abias[...] = rows[:, :BUCKETS] * (1.0 / math.sqrt(4 * DEC))
+    leave(6)
+    spread(rs, DROW, half, aqs, 0, aqs, half)
+    spread(rs, DROW + half, half, aqc, 0, aqc, half)
+    leave(0, 3)
+    for i in range(7):
+        pltpu.make_async_copy(made[i], outs[i], sems.at[i]).wait()
 
 
 def unpack(*arrays):
-    dec = jax.ShapeDtypeStruct((DROW, N * HD), BF)
-    enc = jax.ShapeDtypeStruct((EROW, N * HD), BF)
+    shapes = [(DROW, N * HD)] * 4 + [(EROW, N * HD)] * 2 + [(N, BUCKETS)]
+    kinds = [BF] * 6 + [F32]
     return pl.pallas_call(
         unpack_kernel,
-        out_shape=[dec, dec, dec, dec, enc, enc, jax.ShapeDtypeStruct((N, BUCKETS), F32)],
+        out_shape=[jax.ShapeDtypeStruct(x, t) for x, t in zip(shapes, kinds)],
         in_specs=[VM] * 3,
-        out_specs=[VM] * 7,
+        out_specs=[pl.BlockSpec(memory_space=pl.ANY)] * 7,
+        scratch_shapes=[pltpu.VMEM(x, t) for x, t in zip(shapes, kinds)]
+        + [pltpu.SemaphoreType.DMA((7,))],
         compiler_params=pltpu.CompilerParams(vmem_limit_bytes=16 * 1024 * 1024),
         name="unpack",
     )(*arrays)
@@ -323,7 +360,6 @@
             next_one = next_one + ds[128:256, 256:384]
             far = far + fold(ds[0:128, 256:]) + fold(ds[128:256, 384:])
     bias_out[...] = bucket_sums(near, next_one, far)
-    query_out(dq, gs, DROW)
 
 
 def cross_rows(x4, t3, t4, mk_c, mq, scores, e_c, sg, delta_ref, rg):
@@ -354,15 +390,16 @@
     lax.fori_loop(0, DEC // 256, block, 0)
 
 
-def cross_keys(cu, x4, t4, g3, e_c, sg, delta_ref, rq, rg, dq):
-    rows = pl.ds(pl.multiple_of(cu * 256, 256), 256)
+def cross_keys(first, count, xc, t4, g3, e_c, sg, delta_ref, rq, rg, dq):
+    size = count * EROW
+    rows = pl.ds(pl.multiple_of(first * EROW, EROW), size)
     right = jnp.concatenate([jnp.zeros((HD, DEC), BF), sg[...]], axis=0)
-    dp = dot(x4.part(cu), right)
+    dp = dot(xc[pl.ds(first, count), 0:EROW, :].reshape(size, 128), right)
     e = e_c[rows, :]
     narrow = (e.astype(F32) * (dp - delta_ref[...])).astype(BF)
     part = dot(narrow, rq[...]) + dot(e, rg[...])
-    for i in range(256 // EROW):
-        g3[cu * (256 // EROW) + i] = part[i * EROW : (i + 1) * EROW].astype(BF)
+    for i in range(count):
+        g3[first + i] = part[i * EROW : (i + 1) * EROW].astype(BF)
     dq[...] += dot(t4[0:HD, rows], narrow)
 
 
@@ -372,11 +409,11 @@
     aq, ak, av, ag, bq, bk, bv, bg, dec_v, enc_v, rel_v,
     pc, ps, xc, xs, g3, gs, bias, dp_part, bias_sum,
     t1, t2, t3, t4, mk_s, mk_c, mq, tiles, scores, e_s, e_c, sg, delta_ref, rq, rg, dq,
-    in_sem, send_sem, recv_sem, dp_sem,
+    in_sem, send_sem, recv_sem, dp_sem, up_sem, down_sem, dp_in,
 ):
     me, z, c = place()
     my_dp = lax.axis_index("dp")
-    signal_peers()
+    greet_near()
     loads = []
     pairs = (
         (k_c, bk), (v_c, bv), (q_c, bq), (g_c, bg), (q_s, aq), (k_s, ak), (v_s, av), (g_s, ag),
@@ -401,8 +438,16 @@
         load.wait()
     pack_heads(bk, bv, pc, 0)
     pack_heads(bq, bg, pc, EROW)
-    wait_peers()
-    in_c = send_all(0, pc, xc, STEPS)
+    wait_near()
+    pass_on(up_sem, down_sem, 2)
+    tell(dp_in, dp_peer(1))
+    in_c = send_all(0, pc, xc, NEAR)
+    for hops in (2, 3, 4):
+        heard(up_sem, down_sem, hops)
+        if hops < 4:
+            pass_on(up_sem, down_sem, hops + 1)
+        in_c += send_all(0, pc, xc, at_hops(hops))
+    pl.semaphore_wait(dp_in, 1)
     for load in loads[4:]:
         load.wait()
     pack_heads(aq, ak, ps, 0)
@@ -419,19 +464,33 @@
     x1, x2 = Rows(xs, 0, DROW), Rows(xs, DROW, DROW)
     x3, x4 = Rows(xc, EROW, DROW), Rows(xc, 0, EROW)
 
-    for copy in in_c:
-        copy.wait_recv()
-    turn(x4, t4)
-    turn(x3, t3)
-    left_half(x3, rq)
+    left = left_lanes(2 * DROW)
+    for dz in (0, 1, 7, 2, 6, 3, 5, 4):
+        for copy, step in zip(in_c, IN_ORDER):
+            if step[0] == dz:
+                copy.wait_recv()
+        chip = lax.rem(z + N // 2 - dz, N // 2)
+        block = xc[pl.ds(2 * chip, 2), 0:EROW, :].reshape(2 * EROW, 128)
+        t4[:, pl.ds(pl.multiple_of(chip * 2 * EROW, 2 * EROW), 2 * EROW)] = block.T
+        block = xc[pl.ds(2 * chip, 2), EROW : EROW + DROW, :].reshape(2 * DROW, 128)
+        first = pl.multiple_of(chip * 2 * DROW, 2 * DROW)
+        t3[:, pl.ds(first, 2 * DROW)] = block.T
+        rq[pl.ds(first, 2 * DROW), :] = jnp.where(left, block, 0).astype(BF)
     cross_rows(x4, t3, t4, mk_c, mq, scores, e_c, sg, delta_ref, rg)
     dq[...] = jnp.zeros_like(dq)
     out3, ready = [], []
 
     for dz in (4, 3, 5, 2, 6, 1, 7, 0):
-        cross_keys(lax.rem(z + dz, N // 2), x4, t4, g3, e_c, sg, delta_ref, rq, rg, dq)
-        out3 += send_all(2, g3, r3, ready)
-        ready = [(dz, dc) for dc in (0, 1) if (dz, dc) != (0, 0)]
+        chip = lax.rem(z + dz, N // 2)
+        for first, count in ((0, 1), (1, 1)) if dz == 4 else ((0, 2),):
+            cross_keys(
+                2 * chip + first, count, xc, t4, g3, e_c, sg, delta_ref, rq, rg, dq
+            )
+            out3 += send_all(2, g3, r3, ready)
+            if count == 1:
+                ready = [(dz, lax.rem(c + first, 2))]
+            else:
+                ready = [(dz, dc) for dc in (0, 1) if (dz, dc) != (0, 0)]
     query_out(dq, gs, DROW + DROW // 2)
     out3 += send_all(2, g3, r3, ready)
     r3[me] = g3[me]
@@ -446,26 +505,26 @@
             dst_ref=dp_part.at[my_dp],
             send_sem=dp_sem.at[0, k],
             recv_sem=dp_sem.at[1, k],
-            device_id={"dp": lax.rem(my_dp + k, 4)},
+            device_id=dp_peer(k),
             device_id_type=pl.DeviceIdType.MESH,
         )
         copy.start()
         dp_copies.append(copy)
     dp_part[my_dp] = bias[...]
-    near = [step for step in STEPS if step[0] in (0, 1, 7)]
-    out_s = send_all(3, gs, rs, [step for step in STEPS if step not in near])
+    query_out(dq, gs, DROW)
+    out_s = send_all(3, gs, rs, STEPS[:4])
     rs[me] = gs[me]
     for copy in dp_copies:
         copy.wait()
     total = ((dp_part[0] + dp_part[1]) + dp_part[2]) + dp_part[3]
     bias_sum[...] = total
     rb[me] = total
-    out_s += send_all(3, gs, rs, near[:2])
+    out_s += send_all(3, gs, rs, STEPS[4:6])
     for step in STEPS:
         copy = seq_copy(bias_sum, rb.at[me], send_sem, recv_sem, 4, step)
         copy.start()
         out_s.append(copy)
-    out_s += send_all(3, gs, rs, near[2:])
+    out_s += send_all(3, gs, rs, STEPS[6:])
     for copy in in_c + in_s:
         copy.wait_send()
     for copy in out3 + out_s:
@@ -517,6 +576,9 @@
             pltpu.SemaphoreType.DMA((5, N)),
             pltpu.SemaphoreType.DMA((5, N)),
             pltpu.SemaphoreType.DMA((2, 4)),
+            pltpu.SemaphoreType.REGULAR((5,)),
+            pltpu.SemaphoreType.REGULAR((5,)),
+            pltpu.SemaphoreType.REGULAR,
         ],
         compiler_params=pltpu.CompilerParams(collective_id=0, has_side_effects=True, vmem_limit_bytes=32 * 1024 * 1024
         ),

time: 66.2 us -> 64.7 us (0.977)
  Pallas kernels: 65.4 us -> 64 us
    pallas_call x1, Pallas kernels: 64.2 us -> 62.8 us  [fused(): pl.pallas_call(fused_kernel, out_shape=[jax.ShapeDtypeStruct((N, EROW, 12...]
where the time goes in v4:
time: 64.7 us; the launch traced here: 64.6 us
  Pallas kernels  64 us (99%)
    pallas_call x1, Pallas kernels, fused(): pl.pallas_call(fused_kernel, out_shape=[jax.ShapeDtypeStruct((N, EROW, 12...  62.8 us

profile of v4, /device:TPU:1, one launch (start us, length us, event | category | flops | bytes accessed | tf_op | source)
XLA Modules:
  0.0 64.6 jit_solution(4407703064478985206)
XLA Ops:
  0.6 62.8 %attention_grads.1 = (bf16[16,128,128]{2,1,0:T(8,128)(2,1)S(1)}, bf16[16,128,128]{2,1,0:T(8,128)(2,1)S(1)}, f32[16,1,128]{2,1,0:T(1,128)S(1)}) custom-call(bf16[64,1024]{1,0:T(8,128)(2,1)} %bitcast.18, bf16[64,1024]{1,0:T(8,128)(2,1)} %bitcast.19, bf16[64,1024]{1,0:T(8,128)(2,1)} %bitcast.20, bf16[64,1024]{1,0:T(8,128)(2,1)} %bitcast.21, ...), custom_call_target="tpu_custom_call" | custom-call | tf_op jit(solution)/shard_map/attention_grads/pallas_call | solution.py:536
  63.4 1.2 %unpack.1 = (bf16[64,1024]{1,0:T(8,128)(2,1)}, bf16[64,1024]{1,0:T(8,128)(2,1)}, bf16[64,1024]{1,0:T(8,128)(2,1)}, bf16[64,1024]{1,0:T(8,128)(2,1)}, bf16[128,10...) custom-call(bf16[16,128,128]{2,1,0:T(8,128)(2,1)S(1)} %get-tuple-element.17.r3, ...), custom_call_target="tpu_custom_call" | custom-call | tf_op jit(solution)/shard_map/unpack/pallas_call | solution.py:168

commit v5 on v4

--- a/solution.py
+++ b/solution.py
@@ -128,52 +128,40 @@
         out_ref[2 * pair + 1, span] = jnp.where(left, swap_halves(a), b)
 
 
-def unpack_kernel(
-    r3, rs, rb, dqs, dks, dvs, dqc, dkc, dvc, dbias,
-    aqs, aks, avs, aqc, akc, avc, abias, sems,
-):
-    def spread(src, first, rows, left_out, left_row, right_out, right_row):
-        left = left_lanes(rows)
-        span = slice(first, first + rows)
-        for pair in range(N // 2):
-            a, b = src[2 * pair, span], src[2 * pair + 1, span]
-            lanes = slice(pair * 128, pair * 128 + 128)
-            left_out[left_row : left_row + rows, lanes] = jnp.where(left, a, swap_halves(b))
-            right_out[right_row : right_row + rows, lanes] = jnp.where(left, swap_halves(a), b)
-
-    def leave(*which):
-        for i in which:
-            pltpu.make_async_copy(made[i], outs[i], sems.at[i]).start()
-
-    half = DROW // 2
-    outs = (dqs, dks, dvs, dqc, dkc, dvc, dbias)
-    made = (aqs, aks, avs, aqc, akc, avc, abias)
-    spread(r3, 0, EROW, akc, 0, avc, 0)
-    leave(4, 5)
-    spread(rs, 0, DROW, aks, 0, avs, 0)
-    leave(1, 2)
-    rows = jnp.concatenate([rb[i] for i in range(N)], axis=0)
-    abias[...] = rows[:, :BUCKETS] * (1.0 / math.sqrt(4 * DEC))
-    leave(6)
-    spread(rs, DROW, half, aqs, 0, aqs, half)
-    spread(rs, DROW + half, half, aqc, 0, aqc, half)
-    leave(0, 3)
-    for i in range(7):
-        pltpu.make_async_copy(made[i], outs[i], sems.at[i]).wait()
-
-
-def unpack(*arrays):
-    shapes = [(DROW, N * HD)] * 4 + [(EROW, N * HD)] * 2 + [(N, BUCKETS)]
-    kinds = [BF] * 6 + [F32]
+def unpack_chip(src, chip, first, rows, left_out, left_row, right_out, right_row):
+    left = left_lanes(rows)
+    span = slice(first, first + rows)
+    a, b = src[2 * chip, span], src[2 * chip + 1, span]
+    lanes = pl.ds(pl.multiple_of(chip * 128, 128), 128)
+    left_out[left_row : left_row + rows, lanes] = jnp.where(left, a, swap_halves(b))
+    right_out[right_row : right_row + rows, lanes] = jnp.where(left, swap_halves(a), b)
+
+
+OUT_SHAPES = [jax.ShapeDtypeStruct((DROW, N * HD), BF)] * 4 + [
+    jax.ShapeDtypeStruct((EROW, N * HD), BF),
+    jax.ShapeDtypeStruct((EROW, N * HD), BF),
+    jax.ShapeDtypeStruct((N, BUCKETS), F32),
+]
+
+
+def leave_kernel(*refs):
+    made, outs, sems = refs[:7], refs[7:14], refs[14]
+    copies = [pltpu.make_async_copy(made[i], outs[i], sems.at[i]) for i in range(7)]
+    for copy in copies:
+        copy.start()
+    for copy in copies:
+        copy.wait()
+
+
+def leave(*arrays):
     return pl.pallas_call(
-        unpack_kernel,
-        out_shape=[jax.ShapeDtypeStruct(x, t) for x, t in zip(shapes, kinds)],
-        in_specs=[VM] * 3,
+        leave_kernel,
+        out_shape=OUT_SHAPES,
+        in_specs=[VM] * 7,
         out_specs=[pl.BlockSpec(memory_space=pl.ANY)] * 7,
-        scratch_shapes=[pltpu.VMEM(x, t) for x, t in zip(shapes, kinds)]
-        + [pltpu.SemaphoreType.DMA((7,))],
+        scratch_shapes=[pltpu.SemaphoreType.DMA((7,))],
         compiler_params=pltpu.CompilerParams(vmem_limit_bytes=16 * 1024 * 1024),
-        name="unpack",
+        name="leave",
     )(*arrays)
 
 
@@ -405,9 +393,9 @@
 
 def fused_kernel(
     q_s, k_s, v_s, g_s, q_c, k_c, v_c, g_c, dec_len, enc_len, rel_bias,
-    r3, rs, rb,
+    dqs, dks, dvs, dqc, dkc, dvc, dbias,
     aq, ak, av, ag, bq, bk, bv, bg, dec_v, enc_v, rel_v,
-    pc, ps, xc, xs, g3, gs, bias, dp_part, bias_sum,
+    pc, ps, xc, xs, g3, gs, r3, rs, rb, bias, dp_part, bias_sum,
     t1, t2, t3, t4, mk_s, mk_c, mq, tiles, scores, e_s, e_c, sg, delta_ref, rq, rg, dq,
     in_sem, send_sem, recv_sem, dp_sem, up_sem, down_sem, dp_in,
 ):
@@ -512,36 +500,51 @@
         dp_copies.append(copy)
     dp_part[my_dp] = bias[...]
     query_out(dq, gs, DROW)
-    out_s = send_all(3, gs, rs, STEPS[:4])
+    out_s = send_all(3, gs, rs, IN_ORDER[:6])
     rs[me] = gs[me]
     for copy in dp_copies:
         copy.wait()
     total = ((dp_part[0] + dp_part[1]) + dp_part[2]) + dp_part[3]
     bias_sum[...] = total
     rb[me] = total
-    out_s += send_all(3, gs, rs, STEPS[4:6])
+    out_s += send_all(3, gs, rs, IN_ORDER[6:8])
+    out_b = []
     for step in STEPS:
         copy = seq_copy(bias_sum, rb.at[me], send_sem, recv_sem, 4, step)
         copy.start()
-        out_s.append(copy)
-    out_s += send_all(3, gs, rs, STEPS[6:])
-    for copy in in_c + in_s:
+        out_b.append(copy)
+    out_s += send_all(3, gs, rs, IN_ORDER[8:])
+    half = DROW // 2
+    for i, dz in enumerate((4, 3, 5, 2, 6, 1, 7, 0)):
+        for copy in out3[2 * i : 2 * i + 2]:
+            copy.wait_recv()
+        chip = lax.rem(z + N // 2 - dz, N // 2)
+        unpack_chip(r3, chip, 0, EROW, dkc, 0, dvc, 0)
+    for copy in in_c + in_s + out3:
         copy.wait_send()
-    for copy in out3 + out_s:
+    for copy in out_b:
         copy.wait()
+    rows = jnp.concatenate([rb[i] for i in range(N)], axis=0)
+    dbias[...] = rows[:, :BUCKETS] * (1.0 / math.sqrt(4 * DEC))
+    for dz in (0, 1, 7, 2, 6, 3, 5, 4):
+        for copy, step in zip(out_s, IN_ORDER):
+            if step[0] == dz:
+                copy.wait_recv()
+        chip = lax.rem(z + N // 2 - dz, N // 2)
+        unpack_chip(rs, chip, 0, DROW, dks, 0, dvs, 0)
+        unpack_chip(rs, chip, DROW, half, dqs, 0, dqs, half)
+        unpack_chip(rs, chip, DROW + half, half, dqc, 0, dqc, half)
+    for copy in out_s:
+        copy.wait_send()
 
 
 def fused(*arrays):
     vm = pltpu.VMEM
     return pl.pallas_call(
         fused_kernel,
-        out_shape=[
-            jax.ShapeDtypeStruct((N, EROW, 128), BF),
-            jax.ShapeDtypeStruct((N, EROW, 128), BF),
-            jax.ShapeDtypeStruct((N, 1, 128), F32),
-        ],
+        out_shape=OUT_SHAPES,
         in_specs=[pl.BlockSpec(memory_space=pltpu.HBM)] * 11,
-        out_specs=[VM] * 3,
+        out_specs=[VM] * 7,
         scratch_shapes=[
             *[vm((DROW, N * HD), BF)] * 5,
             *[vm((EROW, N * HD), BF)] * 2,
@@ -553,8 +556,8 @@
             vm((N, 2 * DROW, 128), BF),
             vm((N, EROW + DROW, 128), BF),
             vm((N, 2 * DROW, 128), BF),
-            vm((N, EROW, 128), BF),
-            vm((N, 2 * DROW, 128), BF),
+            *[vm((N, EROW, 128), BF)] * 4,
+            vm((N, 1, 128), F32),
             vm((1, 128), F32),
             vm((4, 1, 128), F32),
             vm((1, 128), F32),
@@ -592,7 +595,7 @@
         pltpu.with_memory_space_constraint(x, pltpu.HBM)
         for x in (*flat, dec_len, enc_len, rel_bias.T)
     ]
-    outs = unpack(*fused(*operands))
+    outs = leave(*fused(*operands))
     return tuple(x.reshape((1,) + x.shape) for x in outs[:6]) + (outs[6].T,)
 
 

time: 64.7 us -> 64.2 us (level)
  Pallas kernels: 64 us -> 63.3 us
    pallas_call x2, Pallas kernels: 64 us -> 63.3 us  [the longest x1 62.2 us: fused(): pl.pallas_call(fused_kernel, out_shape=OUT_SHAPES, in_specs=[pl.BlockSpec...]
where the time goes in v5:
time: 64.2 us; the launch traced here: 63.9 us
  Pallas kernels  63.3 us (99%)
    pallas_call x1, Pallas kernels, fused(): pl.pallas_call(fused_kernel, out_shape=OUT_SHAPES, in_specs=[pl.BlockSpec...  62.2 us

profile of v5, /device:TPU:1, one launch (start us, length us, event | category | flops | bytes accessed | tf_op | source)
XLA Modules:
  0.0 63.9 jit_solution(3631553377920782149)
XLA Ops:
  0.6 62.2 %attention_grads.1 = (bf16[64,1024]{1,0:T(8,128)(2,1)S(1)}, bf16[64,1024]{1,0:T(8,128)(2,1)S(1)}, bf16[64,1024]{1,0:T(8,128)(2,1)S(1)}, bf16[64,1024]{1,0:T(8,12...) custom-call(bf16[64,1024]{1,0:T(8,128)(2,1)} %bitcast.18, ...), custom_call_target="tpu_custom_call" | custom-call | tf_op jit(solution)/shard_map/attention_grads/pallas_call | solution.py:543
  62.9 1.0 %leave.1 = (bf16[64,1024]{1,0:T(8,128)(2,1)}, bf16[64,1024]{1,0:T(8,128)(2,1)}, bf16[64,1024]{1,0:T(8,128)(2,1)}, bf16[64,1024]{1,0:T(8,128)(2,1)}, bf16[128,102...) custom-call(bf16[64,1024]{1,0:T(8,128)(2,1)S(1)} %get-tuple-element.21.refs_0_, ...), custom_call_target="tpu_custom_call" | custom-call | tf_op jit(solution)/shard_map/leave/pallas_call | solution.py:157

commit v6 on v5

--- a/solution.py
+++ b/solution.py
@@ -146,7 +146,14 @@
 
 def leave_kernel(*refs):
     made, outs, sems = refs[:7], refs[7:14], refs[14]
-    copies = [pltpu.make_async_copy(made[i], outs[i], sems.at[i]) for i in range(7)]
+    copies = []
+    for i in (4, 5, 0, 1, 2, 3, 6):
+        size = made[i].shape[0] // 2
+        for j in range(2 if i < 6 else 1):
+            span = slice(j * size, j * size + size) if i < 6 else slice(0, N)
+            copies.append(
+                pltpu.make_async_copy(made[i].at[span], outs[i].at[span], sems.at[i, j])
+            )
     for copy in copies:
         copy.start()
     for copy in copies:
@@ -159,7 +166,7 @@
         out_shape=OUT_SHAPES,
         in_specs=[VM] * 7,
         out_specs=[pl.BlockSpec(memory_space=pl.ANY)] * 7,
-        scratch_shapes=[pltpu.SemaphoreType.DMA((7,))],
+        scratch_shapes=[pltpu.SemaphoreType.DMA((7, 2))],
         compiler_params=pltpu.CompilerParams(vmem_limit_bytes=16 * 1024 * 1024),
         name="leave",
     )(*arrays)

time: 64.2 us -> 64.3 us (level)
  no operation moved by 1% of the time
where the time goes in v6:
time: 64.3 us; the launch traced here: 64 us
  Pallas kernels  63.3 us (98%)
    pallas_call x1, Pallas kernels, fused(): pl.pallas_call(fused_kernel, out_shape=OUT_SHAPES, in_specs=[pl.BlockSpec...  62.2 us

profile of v6, /device:TPU:1, one launch (start us, length us, event | category | flops | bytes accessed | tf_op | source)
XLA Modules:
  0.0 64.0 jit_solution(8637283463825114935)
XLA Ops:
  0.6 62.2 %attention_grads.1 = (bf16[64,1024]{1,0:T(8,128)(2,1)S(1)}, bf16[64,1024]{1,0:T(8,128)(2,1)S(1)}, bf16[64,1024]{1,0:T(8,128)(2,1)S(1)}, bf16[64,1024]{1,0:T(8,12...) custom-call(bf16[64,1024]{1,0:T(8,128)(2,1)} %bitcast.18, ...), custom_call_target="tpu_custom_call" | custom-call | tf_op jit(solution)/shard_map/attention_grads/pallas_call | solution.py:550
  62.9 1.1 %leave.1 = (bf16[64,1024]{1,0:T(8,128)(2,1)}, bf16[64,1024]{1,0:T(8,128)(2,1)}, bf16[64,1024]{1,0:T(8,128)(2,1)}, bf16[64,1024]{1,0:T(8,128)(2,1)}, bf16[128,102...) custom-call(bf16[64,1024]{1,0:T(8,128)(2,1)S(1)} %get-tuple-element.21.refs_0_, ...), custom_call_target="tpu_custom_call" | custom-call | tf_op jit(solution)/shard_map/leave/pallas_call | solution.py:164
